TPU v7x, 32 devices: a whole 2x2x4 slice. The times are simulated.
32 devices in a mesh: group: 2 (over x), gx: 16 (over z, y, core).
Axes of the slice: x: 2, y: 2, z: 4, core: 2. Of those that a mesh axis runs over, the one named last changes fastest.
Arguments:
- features: bfloat16 [192, 256, 16, 128], P(('group', 'gx')), parts along dimension 0, may hold values from -6 to 6
- occupancy: int32 [192, 256, 16], P(('group', 'gx')), parts along dimension 0, may hold values from 0 to 3
- heights: int32 [192, 256], P(('group', 'gx')), parts along dimension 0, may hold values from 0 to 16, as said below
- xy_in: bfloat16 [128, 512], replicated, may hold values from -0.5 to 0.5
- xy_out: bfloat16 [512, 128], replicated, may hold values from -0.25 to 0.25
- xz_in: bfloat16 [128, 512], replicated, may hold values from -0.5 to 0.5
- xz_out: bfloat16 [512, 128], replicated, may hold values from -0.25 to 0.25
- yz_in: bfloat16 [128, 512], replicated, may hold values from -0.5 to 0.5
- yz_out: bfloat16 [512, 128], replicated, may hold values from -0.25 to 0.25
- voxel_in: bfloat16 [128, 256], replicated, may hold values from -0.5 to 0.5
- voxel_out: bfloat16 [256, 128], replicated, may hold values from -0.375 to 0.375
Outputs:
- encoded: bfloat16 [192, 256, 16, 128], P(('group', 'gx')), parts along dimension 0
There are 2 independent parts, one for each index of `group`. A program takes and returns all parts, laid end to end along the dimension named above; an argument that names none is the same for every part. Nothing has to cross between parts.
Inputs may be any that keep to these rules, and one draw needn't show every extreme that they name: `heights`: cells of a column with height index below its valid height count.
All inputs are finite; a program needn't handle non-finite values.
Results may differ from a plain program's by a relative error of at most 0.0073.
Values may be sent and summed in bfloat16 or wider, within the bound.
No kernel may reach another device: no remote copies, remote signals or barrier semaphores. Data moves between devices by JAX's collectives and lax.ppermute only.
A program may use at most 64 MiB of HBM per device.

v0:
```python
import functools

import jax
import jax.numpy as jnp
from jax import lax
from jax.experimental import pallas as pl
from jax.experimental.pallas import tpu as pltpu
from jax.sharding import PartitionSpec as P


BF = jnp.bfloat16
F32 = jnp.float32


def radices(n):
    digits, left = [2], n // 2
    while left > 1:
        digits.append(4 if left % 4 == 0 else 2)
        left //= digits[-1]
    return digits


def mask(digit, weight):
    return digit * weight ^ (1 if weight == 2 else 0)


def offset(pos, n):
    off, slower, weight = 0, n, 1
    for digit in radices(n):
        slower //= digit
        value = (pos // slower) % digit
        crossed = jnp.minimum(value, 1) if weight == 2 else 0
        off = off ^ (value * weight) ^ crossed
        weight *= digit
    return off


def silu(half):
    return half + half * jnp.tanh(half)


def mlp(x, w_in, w_out):
    hidden = silu(jnp.dot(x, w_in, preferred_element_type=F32)).astype(BF)
    return jnp.dot(hidden, w_out, preferred_element_type=F32).astype(BF)


def position(off, n):
    pos, slower, weight, core = 0, n, 1, off % 2
    for digit in radices(n):
        slower //= digit
        if weight > 1:
            value = (off // weight) % digit
            pos = pos + value * slower
            core = core ^ jnp.minimum(value, 1) if weight == 2 else core
        weight *= digit
    return pos + core * (n // 2)


def pool_body(
    n, me_ref, feat_hbm, occ_hbm, hgt_hbm, part_ref, xy_ref, xz_ref, feat_ref,
    occ_ref, hgt_ref, by_z_ref, by_cell_ref, wide_ref, picks_ref, scale_ref, seen_ref, xz_acc, feat_sems,
    side_sems,
):
    rows, y_len, zs, chans = feat_ref.shape
    ys = y_len // n
    tiles, cells, _ = wide_ref.shape
    tile_y, lanes, stack = cells // zs, chans, rows * zs
    both = tile_y + zs

    def fetch(t):
        at = pl.ds(t * tile_y, tile_y)
        return pltpu.make_async_copy(feat_hbm.at[:, at], feat_ref.at[:, at], feat_sems.at[t])

    sides = [
        pltpu.make_async_copy(occ_hbm, occ_ref, side_sems.at[0]),
        pltpu.make_async_copy(hgt_hbm, hgt_ref, side_sems.at[1]),
    ]
    for side in sides:
        side.start()
    lax.fori_loop(0, tiles, lambda t, _: fetch(t).start(), None)

    iota = lambda shape, axis: lax.broadcasted_iota(jnp.int32, shape, axis)
    widen = (iota((stack, rows * chans), 0) // zs == iota((stack, rows * chans), 1) // chans).astype(F32).astype(BF)
    same_z = (iota((stack, cells), 0) % zs == iota((stack, cells), 1) % zs).astype(F32)
    same_y = (iota((tile_y, cells), 0) == iota((tile_y, cells), 1) // zs).astype(F32)
    zidx = iota((zs, lanes), 0)
    for side in sides:
        side.wait()

    parts = lanes // tile_y
    spread = (iota((lanes, parts * cells), 0) == iota((lanes, parts * cells), 1) // zs).astype(F32).astype(BF)
    xz_count = [0.0] * rows
    for block in range(y_len // lanes):
        at = slice(block * lanes, (block + 1) * lanes)
        weights = [
            jnp.where(zidx < hgt_ref[x : x + 1, at], occ_ref[x, :, at], 0).astype(F32) for x in range(rows)
        ]
        seen_ref[block] = sum(weights[1:], weights[0])
        xy_count = [jnp.sum(w, axis=0, keepdims=True) for w in weights]
        xy_count += [jnp.zeros((1, lanes), F32)] * (8 - rows % 8)
        scale_ref[at, : len(xy_count)] = lax.rsqrt(1.0 + jnp.concatenate(xy_count, axis=0)).T
        for x in range(rows):
            xz_count[x] = xz_count[x] + jnp.sum(weights[x], axis=1, keepdims=True)
        stacked = jnp.concatenate(weights, axis=0).astype(BF)
        for part in range(parts):
            columns = slice(part * cells, (part + 1) * cells)
            by_z_ref[block * parts + part] = (
                jnp.dot(stacked, spread[:, columns], preferred_element_type=F32) * same_z
            )
    for t in range(tiles):
        by_cell_ref[t] = by_z_ref[t].T.astype(BF)
    for t in range(tiles):
        wide_ref[t] = jnp.dot(by_cell_ref[t], widen, preferred_element_type=F32)
    for t in range(tiles):
        picks = []
        for x in range(rows):
            row_z = by_z_ref[t, x * zs : (x + 1) * zs]
            picks += [jnp.sum(row_z, axis=0, keepdims=True) * same_y, row_z]
        picks_ref[t] = jnp.concatenate(picks, axis=0).astype(BF)

    xz_acc[...] = jnp.zeros_like(xz_acc)
    group = min(ys, tile_y)

    def tile(t, _):
        first = t * tile_y
        fetch(t).wait()
        for g in range(tile_y // group):
            start = first + g * group
            home, inner = position((start // ys) ^ me_ref[0], n), start % ys
            for y in range(group):
                cell = (g * group + y) * zs
                total = None
                for x in range(rows):
                    weight = wide_ref[t, cell : cell + zs, x * chans : (x + 1) * chans]
                    term = feat_ref[x, start + y].astype(F32) * weight
                    total = term if total is None else total + term
                at = y * zs if group == ys else pl.multiple_of((inner + y) * zs, zs)
                part_ref[home, pl.ds(at, zs), :] = total.astype(BF)
            shift = lax.rem(lanes - lax.rem(start - inner, lanes), lanes)
            part_ref[home, ys * zs :, :] = pltpu.roll(seen_ref[start // lanes], shift, 1).astype(BF)
        for x in range(rows):
            pick = slice(x * both, (x + 1) * both)
            cells_x = feat_ref[x, pl.ds(first, tile_y)].reshape(cells, chans)
            sums = jnp.dot(picks_ref[t, pick], cells_x, preferred_element_type=F32)
            scale = scale_ref[pl.ds(pl.multiple_of(first, tile_y), tile_y), x : x + 1]
            pool = (sums[:tile_y] * jnp.broadcast_to(scale, (tile_y, chans))).astype(BF)
            for g in range(tile_y // group):
                start = first + g * group
                at = slice(None) if group == ys else pl.ds(pl.multiple_of(start % ys, group), group)
                xy_ref[start // ys, x, at] = pool[g * group : (g + 1) * group]
            xz_acc[x] += sums[tile_y:]

    lax.fori_loop(0, tiles, tile, None)
    for x in range(rows):
        scale = lax.rsqrt(1.0 + jnp.broadcast_to(xz_count[x], (zs, chans)))
        xz_ref[x] = (xz_acc[x] * scale).astype(BF)


def pools(feat, occ, hgt, me, n):
    rows, y_len, zs, chans = feat.shape
    ys = y_len // n
    tile_y = 256 // zs
    tiles, cells = y_len // tile_y, tile_y * zs
    vmem = pl.BlockSpec(memory_space=pltpu.VMEM)
    hbm = pl.BlockSpec(memory_space=pltpu.MemorySpace.HBM)
    return pl.pallas_call(
        functools.partial(pool_body, n),
        in_specs=[pl.BlockSpec(memory_space=pltpu.SMEM), hbm, hbm, hbm],
        out_specs=[vmem] * 4,
        out_shape=[
            jax.ShapeDtypeStruct((n, ys * zs + zs, chans), BF),
            jax.ShapeDtypeStruct((n, rows, ys, chans), BF),
            jax.ShapeDtypeStruct((rows, zs, chans), BF),
            jax.ShapeDtypeStruct(feat.shape, BF),
        ],
        scratch_shapes=[
            pltpu.VMEM(occ.shape, jnp.int32),
            pltpu.VMEM(hgt.shape, jnp.int32),
            pltpu.VMEM((tiles, rows * zs, cells), F32),
            pltpu.VMEM((tiles, cells, rows * zs), BF),
            pltpu.VMEM((tiles, cells, rows * chans), F32),
            pltpu.VMEM((tiles, rows * (tile_y + zs), cells), BF),
            pltpu.VMEM((y_len, 16), F32),
            pltpu.VMEM((y_len // chans, zs, chans), F32),
            pltpu.VMEM((rows, zs, chans), F32),
            pltpu.SemaphoreType.DMA((tiles,)),
            pltpu.SemaphoreType.DMA((2,)),
        ],
        compiler_params=pltpu.CompilerParams(vmem_limit_bytes=24 << 20),
        cost_estimate=pl.CostEstimate(flops=8 * feat.size, bytes_accessed=2 * feat.size, transcendentals=0),
        name="pools",
    )(me.reshape(1), *(pltpu.with_memory_space_constraint(a, pltpu.MemorySpace.HBM) for a in (feat, occ, hgt)))


def planes_body(xy_ref, xz_ref, xy_in, xy_out, xz_in, xz_out, xy_plane, xz_plane):
    size = min(256, xy_ref.shape[0])
    for r in range(0, xy_ref.shape[0], size):
        xy_plane[r : r + size] = mlp(xy_ref[r : r + size], 0.5 * xy_in[...], xy_out[...])
    xz_plane[...] = mlp(xz_ref[...], 0.5 * xz_in[...], xz_out[...])


def planes(xy_pool, xz_pool, xy_in, xy_out, xz_in, xz_out):
    vmem = pl.BlockSpec(memory_space=pltpu.VMEM)
    flops = 4 * (xy_pool.size + xz_pool.size) * xy_in.shape[1]
    return pl.pallas_call(
        planes_body,
        in_specs=[vmem] * 6,
        out_specs=[vmem] * 2,
        out_shape=[jax.ShapeDtypeStruct(xy_pool.shape, BF), jax.ShapeDtypeStruct(xz_pool.shape, BF)],
        compiler_params=pltpu.CompilerParams(vmem_limit_bytes=8 << 20),
        cost_estimate=pl.CostEstimate(flops=flops, bytes_accessed=1 << 20, transcendentals=0),
        name="planes",
    )(xy_pool, xz_pool, xy_in, xy_out, xz_in, xz_out)


def yz_body(parts, zs, *refs):
    w_in, w_out, out = refs[parts:]
    total = refs[0][...].astype(F32)
    for ref in refs[1:parts]:
        total = total + ref[...].astype(F32)
    cells, chans = out.shape
    scale = lax.rsqrt(1.0 + total[cells:])
    pool = [
        total[r : r + zs] * jnp.broadcast_to(scale[:, y : y + 1], (zs, chans))
        for y, r in enumerate(range(0, cells, zs))
    ]
    out[...] = mlp(jnp.concatenate(pool, axis=0).astype(BF), 0.5 * w_in[...], w_out[...])


def yz_mlp(parts, zs, w_in, w_out):
    vmem = pl.BlockSpec(memory_space=pltpu.VMEM)
    cells, chans = parts[0].shape[0] - zs, parts[0].shape[1]
    return pl.pallas_call(
        functools.partial(yz_body, len(parts), zs),
        in_specs=[vmem] * (len(parts) + 2),
        out_specs=vmem,
        out_shape=jax.ShapeDtypeStruct((cells, chans), BF),
        compiler_params=pltpu.CompilerParams(vmem_limit_bytes=8 << 20),
        cost_estimate=pl.CostEstimate(flops=4 * cells * w_in.size, bytes_accessed=1 << 19, transcendentals=0),
        name="yz_mlp",
    )(*parts, w_in, w_out)


def first_body(feat_ref, xy_ref, xz_ref, w_in, out_ref):
    n, rows, ys, chans = xy_ref.shape
    zs = xz_ref.shape[1]
    half = 0.5 * w_in[...]

    def chunk(c, _):
        for x in range(rows):
            xy = xy_ref[c, x].astype(F32)
            part = feat_ref[x, pl.ds(c * ys, ys)].astype(F32) + xy[:, None, :] + xz_ref[x].astype(F32)[None]
            part = part.reshape(ys * zs, chans).astype(BF)
            out_ref[c, x] = jnp.dot(part, half, preferred_element_type=F32)

    lax.fori_loop(0, n, chunk, None)


def first_layer(feat, xy_plane, xz_plane, w_in):
    n, rows, ys, _ = xy_plane.shape
    vmem = pl.BlockSpec(memory_space=pltpu.VMEM)
    return pl.pallas_call(
        first_body,
        in_specs=[vmem] * 4,
        out_specs=vmem,
        out_shape=jax.ShapeDtypeStruct((n, rows, ys * xz_plane.shape[1], w_in.shape[1]), F32),
        compiler_params=pltpu.CompilerParams(vmem_limit_bytes=8 << 20),
        cost_estimate=pl.CostEstimate(flops=2 * feat.size * w_in.shape[1], bytes_accessed=1 << 20, transcendentals=0),
        name="first_layer",
    )(feat, xy_plane, xz_plane, w_in)


def voxel_body(n, groups, before, last, me_ref, first_ref, w_in, w_out, *refs):
    yz_refs, refs = refs[: len(groups)], refs[len(groups) :]
    if before:
        prev_ref, refs = refs[0], refs[2:]
    out_hbm, done_ref, sems = refs
    _, rows, ys, zs, chans = done_ref.shape
    half = 0.5 * w_in[...]

    def send(source, index, pos, sem):
        at = pl.ds((offset(pos, n) ^ me_ref[0]) * ys, ys)
        return pltpu.make_async_copy(source.at[index], out_hbm.at[:, at], sems.at[sem])

    copies = [send(prev_ref, j, pos, j) for j, pos in enumerate(before)]
    for copy in copies:
        copy.start()
    slot = 0
    for yz_ref, (pos0, count) in zip(yz_refs, groups):

        def chunk(j, _, yz_ref=yz_ref, pos0=pos0, slot=slot):
            home = offset(pos0 + j, n) ^ me_ref[0]
            yz = jnp.dot(yz_ref[j], half, preferred_element_type=F32)
            for x in range(rows):
                hidden = silu(first_ref[home, x] + yz).astype(BF)
                cells = jnp.dot(hidden, w_out[...], preferred_element_type=F32).astype(BF)
                done_ref[slot + j, x] = cells.reshape(ys, zs, chans)
            if last:
                send(done_ref, slot + j, pos0 + j, len(before) + slot + j).start()

        lax.fori_loop(0, count, chunk, None)
        slot += count
    if last:
        slot = 0
        for pos0, count in groups:
            copies += [send(done_ref, slot + j, pos0 + j, len(before) + slot + j) for j in range(count)]
            slot += count
    for copy in copies:
        copy.wait()


def voxels(state, n, groups, yz, last, me, shape, first, w_in, w_out):
    rows, y_len, zs, chans = shape
    ys, size = y_len // n, sum(count for _, count in groups)
    before, extra = ([], []) if state is None else (state[0], list(state[1:]))
    vmem = pl.BlockSpec(memory_space=pltpu.VMEM)
    hbm = pl.BlockSpec(memory_space=pltpu.MemorySpace.HBM)
    done = (size, rows, ys, zs, chans)
    operands = [me.reshape(1), first, w_in, w_out, *yz, *extra]
    sems = pltpu.SemaphoreType.DMA((len(before) + (size if last else 0) or 1,))
    out = pl.pallas_call(
        functools.partial(voxel_body, n, groups, before, last),
        in_specs=[pl.BlockSpec(memory_space=pltpu.SMEM)] + [vmem] * (3 + len(yz)) + [vmem, hbm][: len(extra)],
        out_specs=[hbm] if last else [hbm, vmem],
        out_shape=[jax.ShapeDtypeStruct(shape, BF)] + ([] if last else [jax.ShapeDtypeStruct(done, BF)]),
        scratch_shapes=([pltpu.VMEM(done, BF)] if last else []) + [sems],
        input_output_aliases={len(operands) - 1: 0} if extra else {},
        compiler_params=pltpu.CompilerParams(vmem_limit_bytes=8 << 20, has_side_effects=True),
        cost_estimate=pl.CostEstimate(
            flops=4 * size * rows * ys * zs * w_in.size, bytes_accessed=1 << 20, transcendentals=0
        ),
        name="voxels",
    )(*operands)
    if last:
        return out[0]
    return [pos0 + j for pos0, count in groups for j in range(count)], out[1], out[0]


def swap(value, n, offset):
    return lax.ppermute(value, "gx", [(i, i ^ offset) for i in range(n)])


def per_device(n, features, occupancy, heights, xy_in, xy_out, xz_in, xz_out, yz_in, yz_out, voxel_in, voxel_out):
    zs = features.shape[2]
    me = lax.axis_index("gx")
    parts, xy_pool, xz_pool, feat = pools(features, jnp.swapaxes(occupancy, 1, 2), heights, me, n)
    chans = features.shape[3]
    xy_plane, xz_plane = planes(
        xy_pool.reshape(-1, chans), xz_pool.reshape(-1, chans), xy_in, xy_out, xz_in, xz_out
    )
    first = first_layer(feat, xy_plane.reshape(xy_pool.shape), xz_plane.reshape(xz_pool.shape), voxel_in)

    digits = radices(n)
    weights = [1]
    for digit in digits:
        weights.append(weights[-1] * digit)
    held = parts
    pieces = None
    for stage, digit in enumerate(digits):
        size = held.shape[0] // digit
        pieces = [held[:size]] + [
            swap(held[d * size : (d + 1) * size], n, mask(d, weights[stage])) for d in range(1, digit)
        ]
        if stage == 1:
            pieces, first = lax.optimization_barrier((pieces, first))
        if stage < len(digits) - 1:
            held = sum(piece.astype(F32) for piece in pieces).astype(BF)
    plane = yz_mlp([piece[0] for piece in pieces], zs, yz_in, yz_out)[None]
    call = functools.partial(
        voxels, me=me, shape=features.shape, first=first, w_in=voxel_in, w_out=voxel_out
    )
    sibling, slower, waiting = n // 2, 1, []
    state = call(None, n, [(0, 1)], [plane], False)
    own = state[0]
    for stage, digit in reversed(list(enumerate(digits))[1:]):
        arrived = []
        for d in range(1, digit):
            arrived.append(swap(plane, n, mask(d, weights[stage])))
        if slower == 1:
            arrived, state = lax.optimization_barrier((arrived, state[1:]))
            plane = jnp.concatenate([plane] + arrived, axis=0)
            groups = [(d, 1) for d in range(1, digit)] + [(sibling, digit)]
            passed = swap(plane, n, 1)
            state = call((own, *state), n, groups, arrived + [passed], False)
        else:
            for d, piece in enumerate(arrived, 1):
                piece, *tail = lax.optimization_barrier((piece, *state[1:]))
                state = (state[0], *tail)
                pieces = waiting + [((d * slower, slower), piece)]
                waiting = [((sibling + d * slower, slower), swap(piece, n, 1))]
                state = call(state, n, [g for g, _ in pieces], [p for _, p in pieces], False)
            plane = jnp.concatenate([plane] + arrived, axis=0)
        slower *= digit
    return call(state, n, [g for g, _ in waiting], [p for _, p in waiting], True)


def solution(mesh):
    split = ("group", "gx")
    in_specs = (P(split, None, None, None), P(split, None, None), P(split, None)) + (P(),) * 8
    n = mesh.shape["gx"]

    def body(*args):
        return per_device(n, *args)

    step = jax.shard_map(
        body, mesh=mesh, in_specs=in_specs, out_specs=P(split, None, None, None), check_vma=False
    )
    if len(radices(n)) > 3:
        return step
    return step
```

profile of v0, /device:TPU:0, one launch (start us, length us, event | category | flops | bytes accessed | tf_op | source)
XLA Modules:
  0.0 50.8 jit_solution(6746019481766761060)
XLA Ops:
  0.0 0.0 copy-start.7
  0.0 0.0 copy-start.6
  0.0 6.5 %pools.1 = (bf16[16,272,128]{2,1,0:T(8,128)(2,1)S(1)}, bf16[16,6,16,128]{3,2,1,0:T(8,128)(2,1)S(1)}, bf16[6,16,128]{2,1,0:T(8,128)(2,1)S(1)}, bf16[6,256,16,128]{3,2,1,0:T(8,128)(2,1)S(1)}) custom-call(s32[1]{0:T(128)} %bitcast.me_ref, bf16[6,256,16,128]{3,2,1,0:T(8,128)(2,1)} %feat_hbm.1, s32[6,16,256]{2,1,0:T(8,128)} %bitcast.18, s32[6,256]{1,0:T(8,128)} %hgt_hbm.1), custom_call_target="tpu_custom_call" | custom-call | flops 25165824 | bytes 6291456 | tf_op jit(solution)/shard_map/pools/pallas_call | solution.py:166
  6.5 0.6 %collective-permute-start = (bf16[8,272,128]{2,1,0:T(8,128)(2,1)S(1)}, bf16[8,272,128]{2,1,0:T(8,128)(2,1)S(1)}, u32[]{:S(2)}, u32[]{:S(2)}) collective-permute-start(bf16[8,272,128]{2,1,0:T(8,128)(2,1)S(1)} %slice.25), channel_id=1, source_target_pairs={{0,1},{1,0},{2,3},{3,2},{4,5},{5,4},{6,7},{7,6},{8,9},{9,8},{10,11... | collective-permute-start | bytes 1671176 | tf_op jit(solution)/shard_map/ppermute | solution.py:340
  7.1 0.0 copy-done.7
  7.1 0.0 copy-done.6
  7.1 0.0 copy-done.5
  7.1 0.0 copy-done.4
  7.1 1.7 %planes.1 = (bf16[1536,128]{1,0:T(8,128)(2,1)S(1)}, bf16[96,128]{1,0:T(8,128)(2,1)S(1)}) custom-call(bf16[1536,128]{1,0:T(8,128)(2,1)S(1)} %bitcast.16, bf16[96,128]{1,0:T(8,128)(2,1)S(1)} %bitcast.17, bf16[128,512]{1,0:T(8,128)(2,1)S(1)} %copy-done.4, bf16[512,128]{1,0:T(8,128)(2,1)S(1)} %copy-done.5, bf16[128,512]{1,0:T(8,128)(2,1)S(1)} %copy-done.6, ...), custom_call_target="tpu_custom_call" | custom-call | flops 427819008 | bytes 1048576 | tf_op jit(solution)/shard_map/planes/pallas_call | solution.py:205
  8.8 0.0 collective-permute-done
  8.8 0.2 add_convert_fusion
  9.0 3.7 %collective-permute-start.3 = (bf16[2,272,128]{2,1,0:T(8,128)(2,1)S(1)}, bf16[2,272,128]{2,1,0:T(8,128)(2,1)S(1)}, u32[]{:S(2)}, u32[]{:S(2)}) collective-permute-start(bf16[2,272,128]{2,1,0:T(8,128)(2,1)S(1)} %get-tuple-element.71), channel_id=1, source_target_pairs={{0,7},{1,6},{2,5},{3,4},{4,3},{5,2},{6,1},{7,0},{8,15},{9,14},{10,... | collective-permute-start | bytes 417800 | tf_op jit(solution)/shard_map/ppermute | solution.py:340
  12.7 0.3 collective-permute-start.2
  13.0 0.2 collective-permute-start.1
  13.2 0.0 copy-done
  13.2 5.8 %first_layer.1.first_ref = f32[16,6,256,256]{3,2,1,0:T(8,128)S(1)} custom-call(bf16[6,256,16,128]{3,2,1,0:T(8,128)(2,1)S(1)} %get-tuple-element.39.feat_ref, bf16[16,6,16,128]{3,2,1,0:T(8,128)(2,1)S(1)} %bitcast.13, bf16[6,16,128]{2,1,0:T(8,128)(2,1)S(1)} %bitcast.15, bf16[128,256]{1,0:T(8,128)(2,1)S(1)} %copy-done), custom_call_target="tpu_custom_call" | custom-call | flops 1610612736 | bytes 1048576 | tf_op jit(solution)/shard_map/first_layer/pallas_call | solution.py:262
  19.0 0.0 collective-permute-done.3
  19.0 0.8 %collective-permute-done.2 = bf16[2,272,128]{2,1,0:T(8,128)(2,1)S(1)} collective-permute-done((bf16[2,272,128]{2,1,0:T(8,128)(2,1)S(1)}, bf16[2,272,128]{2,1,0:T(8,128)(2,1)S(1)}, u32[]{:S(2)}, u32[]{:S(2)}) %collective-permute-start.2) | collective-permute-done | bytes 139296 | tf_op jit(solution)/shard_map/ppermute | solution.py:340
  19.8 0.0 collective-permute-done.1
  19.9 0.1 add_convert_fusion.1
  20.0 2.9 %collective-permute-start.4 = (bf16[1,272,128]{2,1,0:T(8,128)(2,1)S(1)}, bf16[1,272,128]{2,1,0:T(8,128)(2,1)S(1)}, u32[]{:S(2)}, u32[]{:S(2)}) collective-permute-start(bf16[1,272,128]{2,1,0:T(8,128)(2,1)S(1)} %get-tuple-element.75), channel_id=1, source_target_pairs={{0,8},{1,9},{2,10},{3,11},{4,12},{5,13},{6,14},{7,15},{8,0},{9,1},... | collective-permute-start | bytes 208904 | tf_op jit(solution)/shard_map/ppermute | solution.py:340
  22.9 4.0 %collective-permute-done.4 = bf16[1,272,128]{2,1,0:T(8,128)(2,1)S(1)} collective-permute-done((bf16[1,272,128]{2,1,0:T(8,128)(2,1)S(1)}, bf16[1,272,128]{2,1,0:T(8,128)(2,1)S(1)}, u32[]{:S(2)}, u32[]{:S(2)}) %collective-permute-start.4) | collective-permute-done | bytes 69664 | tf_op jit(solution)/shard_map/ppermute | solution.py:340
  26.8 0.0 copy-done.2
  26.8 0.0 copy-done.3
  26.8 0.4 yz_mlp.1
  27.3 1.3 %collective-permute-start.5 = (bf16[1,256,128]{2,1,0:T(8,128)(2,1)S(1)}, bf16[1,256,128]{2,1,0:T(8,128)(2,1)S(1)}, u32[]{:S(2)}, u32[]{:S(2)}) collective-permute-start(bf16[1,256,128]{2,1,0:T(8,128)(2,1)S(1)} %bitcast.10), channel_id=1, source_target_pairs={{0,8},{1,9},{2,10},{3,11},{4,12},{5,13},{6,14},{7,15},{8,0},{9,1},... | collective-permute-start | bytes 196616 | tf_op jit(solution)/shard_map/ppermute | solution.py:340
  28.6 0.0 copy-done.1
  28.6 0.6 %voxels.6 = (bf16[6,256,16,128]{3,2,1,0:T(8,128)(2,1)}, bf16[1,6,16,16,128]{4,3,2,1,0:T(8,128)(2,1)S(1)}) custom-call(s32[1]{0:T(128)} %bitcast.me_ref, f32[16,6,256,256]{3,2,1,0:T(8,128)S(1)} %first_layer.1.first_ref, bf16[128,256]{1,0:T(8,128)(2,1)S(1)} %copy-done, bf16[256,128]{1,0:T(8,128)(2,1)S(1)} %copy-done.1, bf16[1,256,128]{2,1,0:T(8,128)(2,1)S(1)} %bitcast.11), custom_call_target="tpu_custom_call" | custom-call | flops 201326592 | bytes 1048576 | tf_op jit(solution)/shard_map/voxels/pallas_call | solution.py:321
  29.2 4.7 %collective-permute-done.5.refs_0_ = bf16[1,256,128]{2,1,0:T(8,128)(2,1)S(1)} collective-permute-done((bf16[1,256,128]{2,1,0:T(8,128)(2,1)S(1)}, bf16[1,256,128]{2,1,0:T(8,128)(2,1)S(1)}, u32[]{:S(2)}, u32[]{:S(2)}) %collective-permute-start.5) | collective-permute-done | bytes 65568 | tf_op jit(solution)/shard_map/ppermute | solution.py:340
  33.9 0.1 collective-permute-start.8
  33.9 1.6 %collective-permute-start.7 = (bf16[2,256,128]{2,1,0:T(8,128)(2,1)S(1)}, bf16[2,256,128]{2,1,0:T(8,128)(2,1)S(1)}, u32[]{:S(2)}, u32[]{:S(2)}) collective-permute-start(bf16[2,256,128]{2,1,0:T(8,128)(2,1)S(1)} %pad_maximum_fusion), channel_id=1, source_target_pairs={{0,3},{1,2},{2,1},{3,0},{4,7},{5,6},{6,5},{7,4},{8,11},{9,10},{10,... | collective-permute-start | bytes 393224 | tf_op jit(solution)/shard_map/ppermute | solution.py:340
  35.5 0.0 collective-permute-start.10
  35.6 0.0 collective-permute-done.8.refs_1_
  35.6 1.7 %voxels.7 = (bf16[6,256,16,128]{3,2,1,0:T(8,128)(2,1)}, bf16[3,6,16,16,128]{4,3,2,1,0:T(8,128)(2,1)S(1)}) custom-call(s32[1]{0:T(128)} %bitcast.me_ref, f32[16,6,256,256]{3,2,1,0:T(8,128)S(1)} %first_layer.1.first_ref, bf16[128,256]{1,0:T(8,128)(2,1)S(1)} %copy-done, bf16[256,128]{1,0:T(8,128)(2,1)S(1)} %copy-done.1, ...), custom_call_target="tpu_custom_call", output_to_operand_aliasing={{0}: (7, {})} | custom-call | flops 603979776 | bytes 1048576 | tf_op jit(solution)/shard_map/voxels/pallas_call | solution.py:321
  37.2 1.9 %collective-permute-done.7.refs_0_ = bf16[2,256,128]{2,1,0:T(8,128)(2,1)S(1)} collective-permute-done((bf16[2,256,128]{2,1,0:T(8,128)(2,1)S(1)}, bf16[2,256,128]{2,1,0:T(8,128)(2,1)S(1)}, u32[]{:S(2)}, u32[]{:S(2)}) %collective-permute-start.7) | collective-permute-done | bytes 131104 | tf_op jit(solution)/shard_map/ppermute | solution.py:340
  39.2 0.7 %collective-permute-start.9 = (bf16[2,256,128]{2,1,0:T(8,128)(2,1)S(1)}, bf16[2,256,128]{2,1,0:T(8,128)(2,1)S(1)}, u32[]{:S(2)}, u32[]{:S(2)}) collective-permute-start(bf16[2,256,128]{2,1,0:T(8,128)(2,1)S(1)} %collective-permute-done.7.refs_0_), channel_id=1, source_target_pairs={{0,1},{1,0},{2,3},{3,2},{4,5},{5,4},{6,7},{7,6},{8,9},{9,8},{10,11... | collective-permute-start | bytes 393224 | tf_op jit(solution)/shard_map/ppermute | solution.py:340
  39.9 0.5 collective-permute-start.6
  40.4 1.2 %voxels.8 = (bf16[6,256,16,128]{3,2,1,0:T(8,128)(2,1)}, bf16[2,6,16,16,128]{4,3,2,1,0:T(8,128)(2,1)S(1)}) custom-call(s32[1]{0:T(128)} %bitcast.me_ref, f32[16,6,256,256]{3,2,1,0:T(8,128)S(1)} %first_layer.1.first_ref, bf16[128,256]{1,0:T(8,128)(2,1)S(1)} %copy-done, bf16[256,128]{1,0:T(8,128)(2,1)S(1)} %copy-done.1, ...), custom_call_target="tpu_custom_call", output_to_operand_aliasing={{0}: (6, {})} | custom-call | flops 402653184 | bytes 1048576 | tf_op jit(solution)/shard_map/voxels/pallas_call | solution.py:321
  41.5 0.0 collective-permute-done.10.refs_1_
  41.5 0.6 %collective-permute-start.12 = (bf16[2,256,128]{2,1,0:T(8,128)(2,1)S(1)}, bf16[2,256,128]{2,1,0:T(8,128)(2,1)S(1)}, u32[]{:S(2)}, u32[]{:S(2)}) collective-permute-start(bf16[2,256,128]{2,1,0:T(8,128)(2,1)S(1)} %collective-permute-done.10.refs_1_), channel_id=1, source_target_pairs={{0,1},{1,0},{2,3},{3,2},{4,5},{5,4},{6,7},{7,6},{8,9},{9,8},{10,11... | collective-permute-start | bytes 393224 | tf_op jit(solution)/shard_map/ppermute | solution.py:340
  42.1 0.0 collective-permute-done.9.refs_0_
  42.1 2.2 %voxels.9 = (bf16[6,256,16,128]{3,2,1,0:T(8,128)(2,1)}, bf16[4,6,16,16,128]{4,3,2,1,0:T(8,128)(2,1)S(1)}) custom-call(s32[1]{0:T(128)} %bitcast.me_ref, f32[16,6,256,256]{3,2,1,0:T(8,128)S(1)} %first_layer.1.first_ref, bf16[128,256]{1,0:T(8,128)(2,1)S(1)} %copy-done, bf16[256,128]{1,0:T(8,128)(2,1)S(1)} %copy-done.1, ...), custom_call_target="tpu_custom_call", output_to_operand_aliasing={{0}: (7, {})} | custom-call | flops 805306368 | bytes 1048576 | tf_op jit(solution)/shard_map/voxels/pallas_call | solution.py:321
  44.4 2.1 %collective-permute-done.6.refs_1_ = bf16[2,256,128]{2,1,0:T(8,128)(2,1)S(1)} collective-permute-done((bf16[2,256,128]{2,1,0:T(8,128)(2,1)S(1)}, bf16[2,256,128]{2,1,0:T(8,128)(2,1)S(1)}, u32[]{:S(2)}, u32[]{:S(2)}) %collective-permute-start.6) | collective-permute-done | bytes 131104 | tf_op jit(solution)/shard_map/ppermute | solution.py:340
  46.4 0.1 collective-permute-start.11
  46.5 0.0 collective-permute-done.12.refs_0_
  46.5 2.3 %voxels.10 = (bf16[6,256,16,128]{3,2,1,0:T(8,128)(2,1)}, bf16[4,6,16,16,128]{4,3,2,1,0:T(8,128)(2,1)S(1)}) custom-call(s32[1]{0:T(128)} %bitcast.me_ref, f32[16,6,256,256]{3,2,1,0:T(8,128)S(1)} %first_layer.1.first_ref, bf16[128,256]{1,0:T(8,128)(2,1)S(1)} %copy-done, bf16[256,128]{1,0:T(8,128)(2,1)S(1)} %copy-done.1, ...), custom_call_target="tpu_custom_call", output_to_operand_aliasing={{0}: (7, {})} | custom-call | flops 805306368 | bytes 1048576 | tf_op jit(solution)/shard_map/voxels/pallas_call | solution.py:321
  48.8 0.0 collective-permute-done.11.refs_0_
  48.8 1.9 %voxels.11 = bf16[6,256,16,128]{3,2,1,0:T(8,128)(2,1)} custom-call(s32[1]{0:T(128)} %bitcast.me_ref, f32[16,6,256,256]{3,2,1,0:T(8,128)S(1)} %first_layer.1.first_ref, bf16[128,256]{1,0:T(8,128)(2,1)S(1)} %copy-done, bf16[256,128]{1,0:T(8,128)(2,1)S(1)} %copy-done.1, ...), custom_call_target="tpu_custom_call", output_to_operand_aliasing={{}: (6, {})} | custom-call | flops 402653184 | bytes 1048576 | tf_op jit(solution)/shard_map/voxels/pallas_call | solution.py:321
  (10 shorter events, 0.1 us)
Async XLA Ops:
  0.0 7.1 %copy-start.7 = (bf16[512,128]{1,0:T(8,128)(2,1)S(1)}, bf16[512,128]{1,0:T(8,128)(2,1)}, u32[]{:S(2)}) copy-start(bf16[512,128]{1,0:T(8,128)(2,1)} %xz_out.1) | copy-start | bytes 393220
  0.0 7.1 %copy-start.6 = (bf16[128,512]{1,0:T(8,128)(2,1)S(1)}, bf16[128,512]{1,0:T(8,128)(2,1)}, u32[]{:S(2)}) copy-start(bf16[128,512]{1,0:T(8,128)(2,1)} %xz_in.1) | copy-start | bytes 393220
  0.0 7.1 %copy-start.5 = (bf16[512,128]{1,0:T(8,128)(2,1)S(1)}, bf16[512,128]{1,0:T(8,128)(2,1)}, u32[]{:S(2)}) copy-start(bf16[512,128]{1,0:T(8,128)(2,1)} %xy_out.1) | copy-start | bytes 393220
  0.0 7.1 %copy-start.4 = (bf16[128,512]{1,0:T(8,128)(2,1)S(1)}, bf16[128,512]{1,0:T(8,128)(2,1)}, u32[]{:S(2)}) copy-start(bf16[128,512]{1,0:T(8,128)(2,1)} %xy_in.1) | copy-start | bytes 393220
  0.0 13.2 %copy-start = (bf16[128,256]{1,0:T(8,128)(2,1)S(1)}, bf16[128,256]{1,0:T(8,128)(2,1)}, u32[]{:S(2)}) copy-start(bf16[128,256]{1,0:T(8,128)(2,1)} %w_in.13) | copy-start | bytes 196612
  6.5 2.3 %collective-permute-start = (bf16[8,272,128]{2,1,0:T(8,128)(2,1)S(1)}, bf16[8,272,128]{2,1,0:T(8,128)(2,1)S(1)}, u32[]{:S(2)}, u32[]{:S(2)}) collective-permute-start(bf16[8,272,128]{2,1,0:T(8,128)(2,1)S(1)} %slice.25), channel_id=1, source_target_pairs={{0,1},{1,0},{2,3},{3,2},{4,5},{5,4},{6,7},{7,6},{8,9},{9,8},{10,11... | collective-permute-start | bytes 1671176 | tf_op jit(solution)/shard_map/ppermute | solution.py:340
  9.0 10.0 %collective-permute-start.3 = (bf16[2,272,128]{2,1,0:T(8,128)(2,1)S(1)}, bf16[2,272,128]{2,1,0:T(8,128)(2,1)S(1)}, u32[]{:S(2)}, u32[]{:S(2)}) collective-permute-start(bf16[2,272,128]{2,1,0:T(8,128)(2,1)S(1)} %get-tuple-element.71), channel_id=1, source_target_pairs={{0,7},{1,6},{2,5},{3,4},{4,3},{5,2},{6,1},{7,0},{8,15},{9,14},{10,... | collective-permute-start | bytes 417800 | tf_op jit(solution)/shard_map/ppermute | solution.py:340
  12.7 7.1 %collective-permute-start.2 = (bf16[2,272,128]{2,1,0:T(8,128)(2,1)S(1)}, bf16[2,272,128]{2,1,0:T(8,128)(2,1)S(1)}, u32[]{:S(2)}, u32[]{:S(2)}) collective-permute-start(bf16[2,272,128]{2,1,0:T(8,128)(2,1)S(1)} %get-tuple-element.72), channel_id=1, source_target_pairs={{0,5},{1,4},{2,7},{3,6},{4,1},{5,0},{6,3},{7,2},{8,13},{9,12},{10,... | collective-permute-start | bytes 417800 | tf_op jit(solution)/shard_map/ppermute | solution.py:340
  13.0 6.9 %collective-permute-start.1 = (bf16[2,272,128]{2,1,0:T(8,128)(2,1)S(1)}, bf16[2,272,128]{2,1,0:T(8,128)(2,1)S(1)}, u32[]{:S(2)}, u32[]{:S(2)}) collective-permute-start(bf16[2,272,128]{2,1,0:T(8,128)(2,1)S(1)} %get-tuple-element.73), channel_id=1, source_target_pairs={{0,3},{1,2},{2,1},{3,0},{4,7},{5,6},{6,5},{7,4},{8,11},{9,10},{10,... | collective-permute-start | bytes 417800 | tf_op jit(solution)/shard_map/ppermute | solution.py:340
  13.2 13.6 %copy-start.2 = (bf16[128,512]{1,0:T(8,128)(2,1)S(1)}, bf16[128,512]{1,0:T(8,128)(2,1)}, u32[]{:S(2)}) copy-start(bf16[128,512]{1,0:T(8,128)(2,1)} %refs_2_.1) | copy-start | bytes 393220
  13.2 13.6 %copy-start.3 = (bf16[512,128]{1,0:T(8,128)(2,1)S(1)}, bf16[512,128]{1,0:T(8,128)(2,1)}, u32[]{:S(2)}) copy-start(bf16[512,128]{1,0:T(8,128)(2,1)} %refs_3_.1) | copy-start | bytes 393220
  13.2 15.4 %copy-start.1 = (bf16[256,128]{1,0:T(8,128)(2,1)S(1)}, bf16[256,128]{1,0:T(8,128)(2,1)}, u32[]{:S(2)}) copy-start(bf16[256,128]{1,0:T(8,128)(2,1)} %w_out.11) | copy-start | bytes 196612
  20.0 6.9 %collective-permute-start.4 = (bf16[1,272,128]{2,1,0:T(8,128)(2,1)S(1)}, bf16[1,272,128]{2,1,0:T(8,128)(2,1)S(1)}, u32[]{:S(2)}, u32[]{:S(2)}) collective-permute-start(bf16[1,272,128]{2,1,0:T(8,128)(2,1)S(1)} %get-tuple-element.75), channel_id=1, source_target_pairs={{0,8},{1,9},{2,10},{3,11},{4,12},{5,13},{6,14},{7,15},{8,0},{9,1},... | collective-permute-start | bytes 208904 | tf_op jit(solution)/shard_map/ppermute | solution.py:340
  27.3 6.6 %collective-permute-start.5 = (bf16[1,256,128]{2,1,0:T(8,128)(2,1)S(1)}, bf16[1,256,128]{2,1,0:T(8,128)(2,1)S(1)}, u32[]{:S(2)}, u32[]{:S(2)}) collective-permute-start(bf16[1,256,128]{2,1,0:T(8,128)(2,1)S(1)} %bitcast.10), channel_id=1, source_target_pairs={{0,8},{1,9},{2,10},{3,11},{4,12},{5,13},{6,14},{7,15},{8,0},{9,1},... | collective-permute-start | bytes 196616 | tf_op jit(solution)/shard_map/ppermute | solution.py:340
  33.9 1.7 %collective-permute-start.8 = (bf16[2,256,128]{2,1,0:T(8,128)(2,1)S(1)}, bf16[2,256,128]{2,1,0:T(8,128)(2,1)S(1)}, u32[]{:S(2)}, u32[]{:S(2)}) collective-permute-start(bf16[2,256,128]{2,1,0:T(8,128)(2,1)S(1)} %pad_maximum_fusion), channel_id=1, source_target_pairs={{0,1},{1,0},{2,3},{3,2},{4,5},{5,4},{6,7},{7,6},{8,9},{9,8},{10,11... | collective-permute-start | bytes 393224 | tf_op jit(solution)/shard_map/ppermute | solution.py:340
  33.9 5.2 %collective-permute-start.7 = (bf16[2,256,128]{2,1,0:T(8,128)(2,1)S(1)}, bf16[2,256,128]{2,1,0:T(8,128)(2,1)S(1)}, u32[]{:S(2)}, u32[]{:S(2)}) collective-permute-start(bf16[2,256,128]{2,1,0:T(8,128)(2,1)S(1)} %pad_maximum_fusion), channel_id=1, source_target_pairs={{0,3},{1,2},{2,1},{3,0},{4,7},{5,6},{6,5},{7,4},{8,11},{9,10},{10,... | collective-permute-start | bytes 393224 | tf_op jit(solution)/shard_map/ppermute | solution.py:340
  35.5 6.0 %collective-permute-start.10 = (bf16[2,256,128]{2,1,0:T(8,128)(2,1)S(1)}, bf16[2,256,128]{2,1,0:T(8,128)(2,1)S(1)}, u32[]{:S(2)}, u32[]{:S(2)}) collective-permute-start(bf16[2,256,128]{2,1,0:T(8,128)(2,1)S(1)} %pad_maximum_fusion), channel_id=1, source_target_pairs={{0,5},{1,4},{2,7},{3,6},{4,1},{5,0},{6,3},{7,2},{8,13},{9,12},{10,... | collective-permute-start | bytes 393224 | tf_op jit(solution)/shard_map/ppermute | solution.py:340
  39.2 2.9 %collective-permute-start.9 = (bf16[2,256,128]{2,1,0:T(8,128)(2,1)S(1)}, bf16[2,256,128]{2,1,0:T(8,128)(2,1)S(1)}, u32[]{:S(2)}, u32[]{:S(2)}) collective-permute-start(bf16[2,256,128]{2,1,0:T(8,128)(2,1)S(1)} %collective-permute-done.7.refs_0_), channel_id=1, source_target_pairs={{0,1},{1,0},{2,3},{3,2},{4,5},{5,4},{6,7},{7,6},{8,9},{9,8},{10,11... | collective-permute-start | bytes 393224 | tf_op jit(solution)/shard_map/ppermute | solution.py:340
  39.9 6.5 %collective-permute-start.6 = (bf16[2,256,128]{2,1,0:T(8,128)(2,1)S(1)}, bf16[2,256,128]{2,1,0:T(8,128)(2,1)S(1)}, u32[]{:S(2)}, u32[]{:S(2)}) collective-permute-start(bf16[2,256,128]{2,1,0:T(8,128)(2,1)S(1)} %pad_maximum_fusion), channel_id=1, source_target_pairs={{0,7},{1,6},{2,5},{3,4},{4,3},{5,2},{6,1},{7,0},{8,15},{9,14},{10,... | collective-permute-start | bytes 393224 | tf_op jit(solution)/shard_map/ppermute | solution.py:340
  41.5 5.0 %collective-permute-start.12 = (bf16[2,256,128]{2,1,0:T(8,128)(2,1)S(1)}, bf16[2,256,128]{2,1,0:T(8,128)(2,1)S(1)}, u32[]{:S(2)}, u32[]{:S(2)}) collective-permute-start(bf16[2,256,128]{2,1,0:T(8,128)(2,1)S(1)} %collective-permute-done.10.refs_1_), channel_id=1, source_target_pairs={{0,1},{1,0},{2,3},{3,2},{4,5},{5,4},{6,7},{7,6},{8,9},{9,8},{10,11... | collective-permute-start | bytes 393224 | tf_op jit(solution)/shard_map/ppermute | solution.py:340
  46.4 2.4 %collective-permute-start.11 = (bf16[2,256,128]{2,1,0:T(8,128)(2,1)S(1)}, bf16[2,256,128]{2,1,0:T(8,128)(2,1)S(1)}, u32[]{:S(2)}, u32[]{:S(2)}) collective-permute-start(bf16[2,256,128]{2,1,0:T(8,128)(2,1)S(1)} %collective-permute-done.6.refs_1_), channel_id=1, source_target_pairs={{0,1},{1,0},{2,3},{3,2},{4,5},{5,4},{6,7},{7,6},{8,9},{9,8},{10,11... | collective-permute-start | bytes 393224 | tf_op jit(solution)/shard_map/ppermute | solution.py:340
where the time goes:
time: 50.9 us; the launch traced here: 50.8 us
  Pallas kernels  24.2 us (48%)
  waiting for transfers between devices  13.5 us (27%)
  starting transfers between devices  12.6 us (25%)
    ppermute x13, waiting for transfers between devices, swap(): return lax.ppermute(value, 'gx', [(i, i ^ offset) for i in range(n)])  13.5 us
    ppermute x13, starting transfers between devices, swap(): return lax.ppermute(value, 'gx', [(i, i ^ offset) for i in range(n)])  12.6 us
    pallas_call x6, Pallas kernels, voxels(): pl.pallas_call(functools.partial(voxel_body, n, groups, before, last), in...  9.87 us
    pallas_call x1, Pallas kernels, pools(): pl.pallas_call(functools.partial(pool_body, n), in_specs=[pl.BlockSpec(me...  6.46 us
    pallas_call x1, Pallas kernels, first_layer(): pl.pallas_call(first_body, in_specs=[vmem] * 4, out_specs=vmem, out_shape...  5.79 us
    pallas_call x1, Pallas kernels, planes(): pl.pallas_call(planes_body, in_specs=[vmem] * 6, out_specs=[vmem] * 2, ou...  1.66 us
  transfers between devices with their start and end apart: 13, of which 5 were waited for; matrix products, arithmetic and copies ran while one was open for 0% of the time, Pallas kernels for 30%

commit v1 on v0

--- a/solution.py
+++ b/solution.py
@@ -215,28 +215,34 @@
 
 def yz_body(parts, zs, *refs):
     w_in, w_out, out = refs[parts:]
-    total = refs[0][...].astype(F32)
-    for ref in refs[1:parts]:
-        total = total + ref[...].astype(F32)
-    cells, chans = out.shape
-    scale = lax.rsqrt(1.0 + total[cells:])
-    pool = [
-        total[r : r + zs] * jnp.broadcast_to(scale[:, y : y + 1], (zs, chans))
-        for y, r in enumerate(range(0, cells, zs))
-    ]
-    out[...] = mlp(jnp.concatenate(pool, axis=0).astype(BF), 0.5 * w_in[...], w_out[...])
+    count, cells, chans = out.shape
+    pools = []
+    for u in range(count):
+        total = refs[0][u].astype(F32)
+        for v in range(1, parts):
+            total = total + refs[v][u ^ v].astype(F32)
+        scale = lax.rsqrt(1.0 + total[cells:])
+        pools += [
+            total[r : r + zs] * jnp.broadcast_to(scale[:, y : y + 1], (zs, chans))
+            for y, r in enumerate(range(0, cells, zs))
+        ]
+    pool = jnp.concatenate(pools, axis=0).astype(BF)
+    out[...] = mlp(pool, 0.5 * w_in[...], w_out[...]).reshape(count, cells, chans)
 
 
 def yz_mlp(parts, zs, w_in, w_out):
     vmem = pl.BlockSpec(memory_space=pltpu.VMEM)
-    cells, chans = parts[0].shape[0] - zs, parts[0].shape[1]
+    count, rows, chans = parts[0].shape
+    cells = rows - zs
     return pl.pallas_call(
         functools.partial(yz_body, len(parts), zs),
         in_specs=[vmem] * (len(parts) + 2),
         out_specs=vmem,
-        out_shape=jax.ShapeDtypeStruct((cells, chans), BF),
+        out_shape=jax.ShapeDtypeStruct((count, cells, chans), BF),
         compiler_params=pltpu.CompilerParams(vmem_limit_bytes=8 << 20),
-        cost_estimate=pl.CostEstimate(flops=4 * cells * w_in.size, bytes_accessed=1 << 19, transcendentals=0),
+        cost_estimate=pl.CostEstimate(
+            flops=4 * count * cells * w_in.size, bytes_accessed=1 << 19, transcendentals=0
+        ),
         name="yz_mlp",
     )(*parts, w_in, w_out)
 
@@ -274,7 +280,7 @@
     yz_refs, refs = refs[: len(groups)], refs[len(groups) :]
     if before:
         prev_ref, refs = refs[0], refs[2:]
-    out_hbm, done_ref, sems = refs
+    out_hbm, done_ref, own_ref, sems = refs
     _, rows, ys, zs, chans = done_ref.shape
     half = 0.5 * w_in[...]
 
@@ -286,15 +292,20 @@
     for copy in copies:
         copy.start()
     slot = 0
+    for yz_ref, (_, count) in zip(yz_refs, groups):
+        both = yz_ref[...].reshape(count * ys * zs, chans)
+        both = jnp.dot(both, half, preferred_element_type=F32)
+        own_ref[slot : slot + count] = both.reshape(count, ys * zs, half.shape[1])
+        slot += count
+    slot = 0
     for yz_ref, (pos0, count) in zip(yz_refs, groups):
 
         def chunk(j, _, yz_ref=yz_ref, pos0=pos0, slot=slot):
             home = offset(pos0 + j, n) ^ me_ref[0]
-            yz = jnp.dot(yz_ref[j], half, preferred_element_type=F32)
-            for x in range(rows):
-                hidden = silu(first_ref[home, x] + yz).astype(BF)
-                cells = jnp.dot(hidden, w_out[...], preferred_element_type=F32).astype(BF)
-                done_ref[slot + j, x] = cells.reshape(ys, zs, chans)
+            for x in range(0, rows, 3):
+                hidden = silu(first_ref[home, x : x + 3] + own_ref[slot + j][None]).astype(BF)
+                cells = jnp.dot(hidden.reshape(3 * ys * zs, -1), w_out[...], preferred_element_type=F32).astype(BF)
+                done_ref[slot + j, x : x + 3] = cells.reshape(3, ys, zs, chans)
             if last:
                 send(done_ref, slot + j, pos0 + j, len(before) + slot + j).start()
 
@@ -323,9 +334,10 @@
         in_specs=[pl.BlockSpec(memory_space=pltpu.SMEM)] + [vmem] * (3 + len(yz)) + [vmem, hbm][: len(extra)],
         out_specs=[hbm] if last else [hbm, vmem],
         out_shape=[jax.ShapeDtypeStruct(shape, BF)] + ([] if last else [jax.ShapeDtypeStruct(done, BF)]),
-        scratch_shapes=([pltpu.VMEM(done, BF)] if last else []) + [sems],
+        scratch_shapes=([pltpu.VMEM(done, BF)] if last else [])
+        + [pltpu.VMEM((size, ys * zs, w_in.shape[1]), F32), sems],
         input_output_aliases={len(operands) - 1: 0} if extra else {},
-        compiler_params=pltpu.CompilerParams(vmem_limit_bytes=8 << 20, has_side_effects=True),
+        compiler_params=pltpu.CompilerParams(vmem_limit_bytes=20 << 20, has_side_effects=True),
         cost_estimate=pl.CostEstimate(
             flops=4 * size * rows * ys * zs * w_in.size, bytes_accessed=1 << 20, transcendentals=0
         ),
@@ -355,41 +367,35 @@
     for digit in digits:
         weights.append(weights[-1] * digit)
     held = parts
-    pieces = None
-    for stage, digit in enumerate(digits):
+    for stage, digit in enumerate(digits[:-1]):
         size = held.shape[0] // digit
         pieces = [held[:size]] + [
             swap(held[d * size : (d + 1) * size], n, mask(d, weights[stage])) for d in range(1, digit)
         ]
         if stage == 1:
             pieces, first = lax.optimization_barrier((pieces, first))
-        if stage < len(digits) - 1:
-            held = sum(piece.astype(F32) for piece in pieces).astype(BF)
-    plane = yz_mlp([piece[0] for piece in pieces], zs, yz_in, yz_out)[None]
-    call = functools.partial(
-        voxels, me=me, shape=features.shape, first=first, w_in=voxel_in, w_out=voxel_out
-    )
-    sibling, slower, waiting = n // 2, 1, []
-    state = call(None, n, [(0, 1)], [plane], False)
-    own = state[0]
-    for stage, digit in reversed(list(enumerate(digits))[1:]):
+        held = sum(piece.astype(F32) for piece in pieces).astype(BF)
+    slower = digits[-1]
+    pieces = [held] + [swap(held, n, mask(d, weights[len(digits) - 1])) for d in range(1, slower)]
+    plane = yz_mlp(pieces, zs, yz_in, yz_out)
+
+    call = functools.partial(voxels, me=me, shape=features.shape, first=first, w_in=voxel_in, w_out=voxel_out)
+    sibling = n // 2
+    passed = swap(plane, n, 1)
+    state = call(None, n, [(0, slower)], [plane], False)
+    state = call(state, n, [(sibling, slower)], [passed], False)
+    waiting = []
+    for stage, digit in reversed(list(enumerate(digits))[1:-1]):
         arrived = []
         for d in range(1, digit):
             arrived.append(swap(plane, n, mask(d, weights[stage])))
-        if slower == 1:
-            arrived, state = lax.optimization_barrier((arrived, state[1:]))
-            plane = jnp.concatenate([plane] + arrived, axis=0)
-            groups = [(d, 1) for d in range(1, digit)] + [(sibling, digit)]
-            passed = swap(plane, n, 1)
-            state = call((own, *state), n, groups, arrived + [passed], False)
-        else:
-            for d, piece in enumerate(arrived, 1):
-                piece, *tail = lax.optimization_barrier((piece, *state[1:]))
-                state = (state[0], *tail)
-                pieces = waiting + [((d * slower, slower), piece)]
-                waiting = [((sibling + d * slower, slower), swap(piece, n, 1))]
-                state = call(state, n, [g for g, _ in pieces], [p for _, p in pieces], False)
-            plane = jnp.concatenate([plane] + arrived, axis=0)
+        for d, piece in enumerate(arrived, 1):
+            piece, *tail = lax.optimization_barrier((piece, *state[1:]))
+            state = (state[0], *tail)
+            pieces = waiting + [((d * slower, slower), piece)]
+            waiting = [((sibling + d * slower, slower), swap(piece, n, 1))]
+            state = call(state, n, [g for g, _ in pieces], [p for _, p in pieces], False)
+        plane = jnp.concatenate([plane] + arrived, axis=0)
         slower *= digit
     return call(state, n, [g for g, _ in waiting], [p for _, p in waiting], True)
 

time: 50.9 us -> 47 us (0.923)
  waiting for transfers between devices: 13.5 us -> 10.5 us
  Pallas kernels: 24.2 us -> 23.4 us
    ppermute x13 -> x12, waiting for transfers between devices: 13.5 us -> 10.5 us  [swap(): return lax.ppermute(value, 'gx', [(i, i ^ offset) for i in range(n)])]
    pallas_call x6, Pallas kernels: 9.87 us -> 8.98 us  [voxels(): pl.pallas_call(functools.partial(voxel_body, n, groups, before, last), in...]
    ppermute x13 -> x12, starting transfers between devices: 12.6 us -> 12.5 us  [swap(): return lax.ppermute(value, 'gx', [(i, i ^ offset) for i in range(n)])]
  transfers between devices with their start and end apart: 13 -> 12, of which waited for: 5 -> 5; matrix products, arithmetic and copies ran while one was open for 0% -> 0% of each run, Pallas kernels for 30% -> 31%
where the time goes in v1:
time: 47 us; the launch traced here: 46.8 us
  Pallas kernels  23.4 us (50%)
  starting transfers between devices  12.5 us (27%)
  waiting for transfers between devices  10.5 us (22%)
    ppermute x12, starting transfers between devices, swap(): return lax.ppermute(value, 'gx', [(i, i ^ offset) for i in range(n)])  12.5 us
    ppermute x12, waiting for transfers between devices, swap(): return lax.ppermute(value, 'gx', [(i, i ^ offset) for i in range(n)])  10.5 us
    pallas_call x6, Pallas kernels, voxels(): pl.pallas_call(functools.partial(voxel_body, n, groups, before, last), in...  8.98 us
    pallas_call x1, Pallas kernels, pools(): pl.pallas_call(functools.partial(pool_body, n), in_specs=[pl.BlockSpec(me...  6.43 us
    pallas_call x1, Pallas kernels, first_layer(): pl.pallas_call(first_body, in_specs=[vmem] * 4, out_specs=vmem, out_shape...  5.8 us
    pallas_call x1, Pallas kernels, planes(): pl.pallas_call(planes_body, in_specs=[vmem] * 6, out_specs=[vmem] * 2, ou...  1.67 us
  transfers between devices with their start and end apart: 12, of which 5 were waited for; matrix products, arithmetic and copies ran while one was open for 0% of the time, Pallas kernels for 31%

profile of v1, /device:TPU:0, one launch (start us, length us, event | category | flops | bytes accessed | tf_op | source)
XLA Modules:
  0.0 46.8 jit_solution(308492667754524312)
XLA Ops:
  0.0 0.0 copy-start.7
  0.0 0.0 copy-start.6
  0.0 0.0 copy-start.5
  0.0 0.0 copy-start.4
  0.0 6.4 %pools.1 = (bf16[16,272,128]{2,1,0:T(8,128)(2,1)S(1)}, bf16[16,6,16,128]{3,2,1,0:T(8,128)(2,1)S(1)}, bf16[6,16,128]{2,1,0:T(8,128)(2,1)S(1)}, bf16[6,256,16,128]{3,2,1,0:T(8,128)(2,1)S(1)}) custom-call(s32[1]{0:T(128)} %bitcast.me_ref, bf16[6,256,16,128]{3,2,1,0:T(8,128)(2,1)} %feat_hbm.1, s32[6,16,256]{2,1,0:T(8,128)} %bitcast.10, s32[6,256]{1,0:T(8,128)} %hgt_hbm.1), custom_call_target="tpu_custom_call" | custom-call | flops 25165824 | bytes 6291456 | tf_op jit(solution)/shard_map/pools/pallas_call | solution.py:166
  6.5 0.6 %collective-permute-start = (bf16[8,272,128]{2,1,0:T(8,128)(2,1)S(1)}, bf16[8,272,128]{2,1,0:T(8,128)(2,1)S(1)}, u32[]{:S(2)}, u32[]{:S(2)}) collective-permute-start(bf16[8,272,128]{2,1,0:T(8,128)(2,1)S(1)} %slice.19), channel_id=1, source_target_pairs={{0,1},{1,0},{2,3},{3,2},{4,5},{5,4},{6,7},{7,6},{8,9},{9,8},{10,11... | collective-permute-start | bytes 1671176 | tf_op jit(solution)/shard_map/ppermute | solution.py:352
  7.1 0.0 copy-done.7
  7.1 0.0 copy-done.6
  7.1 0.0 copy-done.5
  7.1 0.0 copy-done.4
  7.1 1.7 %planes.1 = (bf16[1536,128]{1,0:T(8,128)(2,1)S(1)}, bf16[96,128]{1,0:T(8,128)(2,1)S(1)}) custom-call(bf16[1536,128]{1,0:T(8,128)(2,1)S(1)} %bitcast.8, bf16[96,128]{1,0:T(8,128)(2,1)S(1)} %bitcast.9, bf16[128,512]{1,0:T(8,128)(2,1)S(1)} %copy-done.4, bf16[512,128]{1,0:T(8,128)(2,1)S(1)} %copy-done.5, bf16[128,512]{1,0:T(8,128)(2,1)S(1)} %copy-done.6, ...), custom_call_target="tpu_custom_call" | custom-call | flops 427819008 | bytes 1048576 | tf_op jit(solution)/shard_map/planes/pallas_call | solution.py:205
  8.8 0.0 collective-permute-done
  8.8 0.2 add_convert_fusion
  9.0 3.7 %collective-permute-start.3 = (bf16[2,272,128]{2,1,0:T(8,128)(2,1)S(1)}, bf16[2,272,128]{2,1,0:T(8,128)(2,1)S(1)}, u32[]{:S(2)}, u32[]{:S(2)}) collective-permute-start(bf16[2,272,128]{2,1,0:T(8,128)(2,1)S(1)} %get-tuple-element.65), channel_id=1, source_target_pairs={{0,7},{1,6},{2,5},{3,4},{4,3},{5,2},{6,1},{7,0},{8,15},{9,14},{10,... | collective-permute-start | bytes 417800 | tf_op jit(solution)/shard_map/ppermute | solution.py:352
  12.7 0.3 collective-permute-start.2
  13.0 0.2 collective-permute-start.1
  13.2 0.0 copy-done
  13.2 5.8 %first_layer.1.first_ref = f32[16,6,256,256]{3,2,1,0:T(8,128)S(1)} custom-call(bf16[6,256,16,128]{3,2,1,0:T(8,128)(2,1)S(1)} %get-tuple-element.36.feat_ref, bf16[16,6,16,128]{3,2,1,0:T(8,128)(2,1)S(1)} %bitcast.6, bf16[6,16,128]{2,1,0:T(8,128)(2,1)S(1)} %bitcast.7, bf16[128,256]{1,0:T(8,128)(2,1)S(1)} %copy-done), custom_call_target="tpu_custom_call" | custom-call | flops 1610612736 | bytes 1048576 | tf_op jit(solution)/shard_map/first_layer/pallas_call | solution.py:268
  19.0 0.0 collective-permute-done.3
  19.0 0.8 %collective-permute-done.2 = bf16[2,272,128]{2,1,0:T(8,128)(2,1)S(1)} collective-permute-done((bf16[2,272,128]{2,1,0:T(8,128)(2,1)S(1)}, bf16[2,272,128]{2,1,0:T(8,128)(2,1)S(1)}, u32[]{:S(2)}, u32[]{:S(2)}) %collective-permute-start.2) | collective-permute-done | bytes 139296 | tf_op jit(solution)/shard_map/ppermute | solution.py:352
  19.8 0.1 collective-permute-done.1
  19.9 0.1 add_convert_fusion.1.refs_0_
  19.9 2.9 %collective-permute-start.4 = (bf16[2,272,128]{2,1,0:T(8,128)(2,1)S(1)}, bf16[2,272,128]{2,1,0:T(8,128)(2,1)S(1)}, u32[]{:S(2)}, u32[]{:S(2)}) collective-permute-start(bf16[2,272,128]{2,1,0:T(8,128)(2,1)S(1)} %add_convert_fusion.1.refs_0_), channel_id=1, source_target_pairs={{0,8},{1,9},{2,10},{3,11},{4,12},{5,13},{6,14},{7,15},{8,0},{9,1},... | collective-permute-start | bytes 417800 | tf_op jit(solution)/shard_map/ppermute | solution.py:352
  22.8 6.9 %collective-permute-done.4.refs_1_ = bf16[2,272,128]{2,1,0:T(8,128)(2,1)S(1)} collective-permute-done((bf16[2,272,128]{2,1,0:T(8,128)(2,1)S(1)}, bf16[2,272,128]{2,1,0:T(8,128)(2,1)S(1)}, u32[]{:S(2)}, u32[]{:S(2)}) %collective-permute-start.4) | collective-permute-done | bytes 139296 | tf_op jit(solution)/shard_map/ppermute | solution.py:352
  29.8 0.0 copy-done.2
  29.8 0.0 copy-done.3
  29.8 0.5 %yz_mlp.1.refs_0_ = bf16[2,256,128]{2,1,0:T(8,128)(2,1)S(1)} custom-call(bf16[2,272,128]{2,1,0:T(8,128)(2,1)S(1)} %add_convert_fusion.1.refs_0_, bf16[2,272,128]{2,1,0:T(8,128)(2,1)S(1)} %collective-permute-done.4.refs_1_, bf16[128,512]{1,0:T(8,128)(2,1)S(1)} %copy-done.2, bf16[512,128]{1,0:T(8,128)(2,1)S(1)} %copy-done.3), custom_call_target="tpu_custom_call" | custom-call | flops 134217728 | bytes 524288 | tf_op jit(solution)/shard_map/yz_mlp/pallas_call | solution.py:237
  30.3 0.1 collective-permute-start.7
  30.4 1.7 %collective-permute-start.6 = (bf16[2,256,128]{2,1,0:T(8,128)(2,1)S(1)}, bf16[2,256,128]{2,1,0:T(8,128)(2,1)S(1)}, u32[]{:S(2)}, u32[]{:S(2)}) collective-permute-start(bf16[2,256,128]{2,1,0:T(8,128)(2,1)S(1)} %yz_mlp.1.refs_0_), channel_id=1, source_target_pairs={{0,3},{1,2},{2,1},{3,0},{4,7},{5,6},{6,5},{7,4},{8,11},{9,10},{10,... | collective-permute-start | bytes 393224 | tf_op jit(solution)/shard_map/ppermute | solution.py:352
  32.0 0.4 collective-permute-start.9
  32.4 0.0 copy-done.1
  32.4 1.0 %voxels.6 = (bf16[6,256,16,128]{3,2,1,0:T(8,128)(2,1)}, bf16[2,6,16,16,128]{4,3,2,1,0:T(8,128)(2,1)S(1)}) custom-call(s32[1]{0:T(128)} %bitcast.me_ref, f32[16,6,256,256]{3,2,1,0:T(8,128)S(1)} %first_layer.1.first_ref, bf16[128,256]{1,0:T(8,128)(2,1)S(1)} %copy-done, bf16[256,128]{1,0:T(8,128)(2,1)S(1)} %copy-done.1, bf16[2,256,128]{2,1,0:T(8,128)(2,1)S(1)} %yz_mlp.1.refs_0_), custom_call_target="tpu_custom_call" | custom-call | flops 402653184 | bytes 1048576 | tf_op jit(solution)/shard_map/voxels/pallas_call | solution.py:332
  33.5 0.0 collective-permute-done.7.refs_0_
  33.5 1.1 %voxels.7 = (bf16[6,256,16,128]{3,2,1,0:T(8,128)(2,1)}, bf16[2,6,16,16,128]{4,3,2,1,0:T(8,128)(2,1)S(1)}) custom-call(s32[1]{0:T(128)} %bitcast.me_ref, f32[16,6,256,256]{3,2,1,0:T(8,128)S(1)} %first_layer.1.first_ref, bf16[128,256]{1,0:T(8,128)(2,1)S(1)} %copy-done, bf16[256,128]{1,0:T(8,128)(2,1)S(1)} %copy-done.1, ...), custom_call_target="tpu_custom_call", output_to_operand_aliasing={{0}: (6, {})} | custom-call | flops 402653184 | bytes 1048576 | tf_op jit(solution)/shard_map/voxels/pallas_call | solution.py:332
  34.5 1.1 %collective-permute-done.6.refs_0_ = bf16[2,256,128]{2,1,0:T(8,128)(2,1)S(1)} collective-permute-done((bf16[2,256,128]{2,1,0:T(8,128)(2,1)S(1)}, bf16[2,256,128]{2,1,0:T(8,128)(2,1)S(1)}, u32[]{:S(2)}, u32[]{:S(2)}) %collective-permute-start.6) | collective-permute-done | bytes 131104 | tf_op jit(solution)/shard_map/ppermute | solution.py:352
  35.6 0.7 %collective-permute-start.8 = (bf16[2,256,128]{2,1,0:T(8,128)(2,1)S(1)}, bf16[2,256,128]{2,1,0:T(8,128)(2,1)S(1)}, u32[]{:S(2)}, u32[]{:S(2)}) collective-permute-start(bf16[2,256,128]{2,1,0:T(8,128)(2,1)S(1)} %collective-permute-done.6.refs_0_), channel_id=1, source_target_pairs={{0,1},{1,0},{2,3},{3,2},{4,5},{5,4},{6,7},{7,6},{8,9},{9,8},{10,11... | collective-permute-start | bytes 393224 | tf_op jit(solution)/shard_map/ppermute | solution.py:352
  36.3 1.3 %collective-permute-start.5 = (bf16[2,256,128]{2,1,0:T(8,128)(2,1)S(1)}, bf16[2,256,128]{2,1,0:T(8,128)(2,1)S(1)}, u32[]{:S(2)}, u32[]{:S(2)}) collective-permute-start(bf16[2,256,128]{2,1,0:T(8,128)(2,1)S(1)} %yz_mlp.1.refs_0_), channel_id=1, source_target_pairs={{0,7},{1,6},{2,5},{3,4},{4,3},{5,2},{6,1},{7,0},{8,15},{9,14},{10,... | collective-permute-start | bytes 393224 | tf_op jit(solution)/shard_map/ppermute | solution.py:352
  37.6 1.1 %voxels.8 = (bf16[6,256,16,128]{3,2,1,0:T(8,128)(2,1)}, bf16[2,6,16,16,128]{4,3,2,1,0:T(8,128)(2,1)S(1)}) custom-call(s32[1]{0:T(128)} %bitcast.me_ref, f32[16,6,256,256]{3,2,1,0:T(8,128)S(1)} %first_layer.1.first_ref, bf16[128,256]{1,0:T(8,128)(2,1)S(1)} %copy-done, bf16[256,128]{1,0:T(8,128)(2,1)S(1)} %copy-done.1, ...), custom_call_target="tpu_custom_call", output_to_operand_aliasing={{0}: (6, {})} | custom-call | flops 402653184 | bytes 1048576 | tf_op jit(solution)/shard_map/voxels/pallas_call | solution.py:332
  38.7 0.0 collective-permute-done.9.refs_1_
  38.7 0.6 %collective-permute-start.11 = (bf16[2,256,128]{2,1,0:T(8,128)(2,1)S(1)}, bf16[2,256,128]{2,1,0:T(8,128)(2,1)S(1)}, u32[]{:S(2)}, u32[]{:S(2)}) collective-permute-start(bf16[2,256,128]{2,1,0:T(8,128)(2,1)S(1)} %collective-permute-done.9.refs_1_), channel_id=1, source_target_pairs={{0,1},{1,0},{2,3},{3,2},{4,5},{5,4},{6,7},{7,6},{8,9},{9,8},{10,11... | collective-permute-start | bytes 393224 | tf_op jit(solution)/shard_map/ppermute | solution.py:352
  39.3 0.0 collective-permute-done.8.refs_0_
  39.3 2.0 %voxels.9 = (bf16[6,256,16,128]{3,2,1,0:T(8,128)(2,1)}, bf16[4,6,16,16,128]{4,3,2,1,0:T(8,128)(2,1)S(1)}) custom-call(s32[1]{0:T(128)} %bitcast.me_ref, f32[16,6,256,256]{3,2,1,0:T(8,128)S(1)} %first_layer.1.first_ref, bf16[128,256]{1,0:T(8,128)(2,1)S(1)} %copy-done, bf16[256,128]{1,0:T(8,128)(2,1)S(1)} %copy-done.1, ...), custom_call_target="tpu_custom_call", output_to_operand_aliasing={{0}: (7, {})} | custom-call | flops 805306368 | bytes 1048576 | tf_op jit(solution)/shard_map/voxels/pallas_call | solution.py:332
  41.3 1.6 %collective-permute-done.5.refs_1_ = bf16[2,256,128]{2,1,0:T(8,128)(2,1)S(1)} collective-permute-done((bf16[2,256,128]{2,1,0:T(8,128)(2,1)S(1)}, bf16[2,256,128]{2,1,0:T(8,128)(2,1)S(1)}, u32[]{:S(2)}, u32[]{:S(2)}) %collective-permute-start.5) | collective-permute-done | bytes 131104 | tf_op jit(solution)/shard_map/ppermute | solution.py:352
  42.9 0.1 collective-permute-start.10
  43.0 0.0 collective-permute-done.11.refs_0_
  43.0 2.0 %voxels.10 = (bf16[6,256,16,128]{3,2,1,0:T(8,128)(2,1)}, bf16[4,6,16,16,128]{4,3,2,1,0:T(8,128)(2,1)S(1)}) custom-call(s32[1]{0:T(128)} %bitcast.me_ref, f32[16,6,256,256]{3,2,1,0:T(8,128)S(1)} %first_layer.1.first_ref, bf16[128,256]{1,0:T(8,128)(2,1)S(1)} %copy-done, bf16[256,128]{1,0:T(8,128)(2,1)S(1)} %copy-done.1, ...), custom_call_target="tpu_custom_call", output_to_operand_aliasing={{0}: (7, {})} | custom-call | flops 805306368 | bytes 1048576 | tf_op jit(solution)/shard_map/voxels/pallas_call | solution.py:332
  45.0 0.0 collective-permute-done.10.refs_0_
  45.0 1.8 %voxels.11 = bf16[6,256,16,128]{3,2,1,0:T(8,128)(2,1)} custom-call(s32[1]{0:T(128)} %bitcast.me_ref, f32[16,6,256,256]{3,2,1,0:T(8,128)S(1)} %first_layer.1.first_ref, bf16[128,256]{1,0:T(8,128)(2,1)S(1)} %copy-done, bf16[256,128]{1,0:T(8,128)(2,1)S(1)} %copy-done.1, ...), custom_call_target="tpu_custom_call", output_to_operand_aliasing={{}: (6, {})} | custom-call | flops 402653184 | bytes 1048576 | tf_op jit(solution)/shard_map/voxels/pallas_call | solution.py:332
  (6 shorter events, 0.1 us)
Async XLA Ops:
  0.0 7.1 %copy-start.7 = (bf16[512,128]{1,0:T(8,128)(2,1)S(1)}, bf16[512,128]{1,0:T(8,128)(2,1)}, u32[]{:S(2)}) copy-start(bf16[512,128]{1,0:T(8,128)(2,1)} %xz_out.1) | copy-start | bytes 393220
  0.0 7.1 %copy-start.6 = (bf16[128,512]{1,0:T(8,128)(2,1)S(1)}, bf16[128,512]{1,0:T(8,128)(2,1)}, u32[]{:S(2)}) copy-start(bf16[128,512]{1,0:T(8,128)(2,1)} %xz_in.1) | copy-start | bytes 393220
  0.0 7.1 %copy-start.5 = (bf16[512,128]{1,0:T(8,128)(2,1)S(1)}, bf16[512,128]{1,0:T(8,128)(2,1)}, u32[]{:S(2)}) copy-start(bf16[512,128]{1,0:T(8,128)(2,1)} %xy_out.1) | copy-start | bytes 393220
  0.0 7.1 %copy-start.4 = (bf16[128,512]{1,0:T(8,128)(2,1)S(1)}, bf16[128,512]{1,0:T(8,128)(2,1)}, u32[]{:S(2)}) copy-start(bf16[128,512]{1,0:T(8,128)(2,1)} %xy_in.1) | copy-start | bytes 393220
  0.0 13.2 %copy-start = (bf16[128,256]{1,0:T(8,128)(2,1)S(1)}, bf16[128,256]{1,0:T(8,128)(2,1)}, u32[]{:S(2)}) copy-start(bf16[128,256]{1,0:T(8,128)(2,1)} %w_in.13) | copy-start | bytes 196612
  6.5 2.3 %collective-permute-start = (bf16[8,272,128]{2,1,0:T(8,128)(2,1)S(1)}, bf16[8,272,128]{2,1,0:T(8,128)(2,1)S(1)}, u32[]{:S(2)}, u32[]{:S(2)}) collective-permute-start(bf16[8,272,128]{2,1,0:T(8,128)(2,1)S(1)} %slice.19), channel_id=1, source_target_pairs={{0,1},{1,0},{2,3},{3,2},{4,5},{5,4},{6,7},{7,6},{8,9},{9,8},{10,11... | collective-permute-start | bytes 1671176 | tf_op jit(solution)/shard_map/ppermute | solution.py:352
  9.0 10.0 %collective-permute-start.3 = (bf16[2,272,128]{2,1,0:T(8,128)(2,1)S(1)}, bf16[2,272,128]{2,1,0:T(8,128)(2,1)S(1)}, u32[]{:S(2)}, u32[]{:S(2)}) collective-permute-start(bf16[2,272,128]{2,1,0:T(8,128)(2,1)S(1)} %get-tuple-element.65), channel_id=1, source_target_pairs={{0,7},{1,6},{2,5},{3,4},{4,3},{5,2},{6,1},{7,0},{8,15},{9,14},{10,... | collective-permute-start | bytes 417800 | tf_op jit(solution)/shard_map/ppermute | solution.py:352
  12.7 7.1 %collective-permute-start.2 = (bf16[2,272,128]{2,1,0:T(8,128)(2,1)S(1)}, bf16[2,272,128]{2,1,0:T(8,128)(2,1)S(1)}, u32[]{:S(2)}, u32[]{:S(2)}) collective-permute-start(bf16[2,272,128]{2,1,0:T(8,128)(2,1)S(1)} %get-tuple-element.66), channel_id=1, source_target_pairs={{0,5},{1,4},{2,7},{3,6},{4,1},{5,0},{6,3},{7,2},{8,13},{9,12},{10,... | collective-permute-start | bytes 417800 | tf_op jit(solution)/shard_map/ppermute | solution.py:352
  13.0 6.9 %collective-permute-start.1 = (bf16[2,272,128]{2,1,0:T(8,128)(2,1)S(1)}, bf16[2,272,128]{2,1,0:T(8,128)(2,1)S(1)}, u32[]{:S(2)}, u32[]{:S(2)}) collective-permute-start(bf16[2,272,128]{2,1,0:T(8,128)(2,1)S(1)} %get-tuple-element.67), channel_id=1, source_target_pairs={{0,3},{1,2},{2,1},{3,0},{4,7},{5,6},{6,5},{7,4},{8,11},{9,10},{10,... | collective-permute-start | bytes 417800 | tf_op jit(solution)/shard_map/ppermute | solution.py:352
  13.2 16.6 %copy-start.2 = (bf16[128,512]{1,0:T(8,128)(2,1)S(1)}, bf16[128,512]{1,0:T(8,128)(2,1)}, u32[]{:S(2)}) copy-start(bf16[128,512]{1,0:T(8,128)(2,1)} %refs_2_.1) | copy-start | bytes 393220
  13.2 16.6 %copy-start.3 = (bf16[512,128]{1,0:T(8,128)(2,1)S(1)}, bf16[512,128]{1,0:T(8,128)(2,1)}, u32[]{:S(2)}) copy-start(bf16[512,128]{1,0:T(8,128)(2,1)} %refs_3_.1) | copy-start | bytes 393220
  13.2 19.2 %copy-start.1 = (bf16[256,128]{1,0:T(8,128)(2,1)S(1)}, bf16[256,128]{1,0:T(8,128)(2,1)}, u32[]{:S(2)}) copy-start(bf16[256,128]{1,0:T(8,128)(2,1)} %w_out.11) | copy-start | bytes 196612
  19.9 9.8 %collective-permute-start.4 = (bf16[2,272,128]{2,1,0:T(8,128)(2,1)S(1)}, bf16[2,272,128]{2,1,0:T(8,128)(2,1)S(1)}, u32[]{:S(2)}, u32[]{:S(2)}) collective-permute-start(bf16[2,272,128]{2,1,0:T(8,128)(2,1)S(1)} %add_convert_fusion.1.refs_0_), channel_id=1, source_target_pairs={{0,8},{1,9},{2,10},{3,11},{4,12},{5,13},{6,14},{7,15},{8,0},{9,1},... | collective-permute-start | bytes 417800 | tf_op jit(solution)/shard_map/ppermute | solution.py:352
  30.3 3.2 %collective-permute-start.7 = (bf16[2,256,128]{2,1,0:T(8,128)(2,1)S(1)}, bf16[2,256,128]{2,1,0:T(8,128)(2,1)S(1)}, u32[]{:S(2)}, u32[]{:S(2)}) collective-permute-start(bf16[2,256,128]{2,1,0:T(8,128)(2,1)S(1)} %yz_mlp.1.refs_0_), channel_id=1, source_target_pairs={{0,1},{1,0},{2,3},{3,2},{4,5},{5,4},{6,7},{7,6},{8,9},{9,8},{10,11... | collective-permute-start | bytes 393224 | tf_op jit(solution)/shard_map/ppermute | solution.py:352
  30.4 5.2 %collective-permute-start.6 = (bf16[2,256,128]{2,1,0:T(8,128)(2,1)S(1)}, bf16[2,256,128]{2,1,0:T(8,128)(2,1)S(1)}, u32[]{:S(2)}, u32[]{:S(2)}) collective-permute-start(bf16[2,256,128]{2,1,0:T(8,128)(2,1)S(1)} %yz_mlp.1.refs_0_), channel_id=1, source_target_pairs={{0,3},{1,2},{2,1},{3,0},{4,7},{5,6},{6,5},{7,4},{8,11},{9,10},{10,... | collective-permute-start | bytes 393224 | tf_op jit(solution)/shard_map/ppermute | solution.py:352
  32.0 6.7 %collective-permute-start.9 = (bf16[2,256,128]{2,1,0:T(8,128)(2,1)S(1)}, bf16[2,256,128]{2,1,0:T(8,128)(2,1)S(1)}, u32[]{:S(2)}, u32[]{:S(2)}) collective-permute-start(bf16[2,256,128]{2,1,0:T(8,128)(2,1)S(1)} %yz_mlp.1.refs_0_), channel_id=1, source_target_pairs={{0,5},{1,4},{2,7},{3,6},{4,1},{5,0},{6,3},{7,2},{8,13},{9,12},{10,... | collective-permute-start | bytes 393224 | tf_op jit(solution)/shard_map/ppermute | solution.py:352
  35.6 3.7 %collective-permute-start.8 = (bf16[2,256,128]{2,1,0:T(8,128)(2,1)S(1)}, bf16[2,256,128]{2,1,0:T(8,128)(2,1)S(1)}, u32[]{:S(2)}, u32[]{:S(2)}) collective-permute-start(bf16[2,256,128]{2,1,0:T(8,128)(2,1)S(1)} %collective-permute-done.6.refs_0_), channel_id=1, source_target_pairs={{0,1},{1,0},{2,3},{3,2},{4,5},{5,4},{6,7},{7,6},{8,9},{9,8},{10,11... | collective-permute-start | bytes 393224 | tf_op jit(solution)/shard_map/ppermute | solution.py:352
  36.3 6.5 %collective-permute-start.5 = (bf16[2,256,128]{2,1,0:T(8,128)(2,1)S(1)}, bf16[2,256,128]{2,1,0:T(8,128)(2,1)S(1)}, u32[]{:S(2)}, u32[]{:S(2)}) collective-permute-start(bf16[2,256,128]{2,1,0:T(8,128)(2,1)S(1)} %yz_mlp.1.refs_0_), channel_id=1, source_target_pairs={{0,7},{1,6},{2,5},{3,4},{4,3},{5,2},{6,1},{7,0},{8,15},{9,14},{10,... | collective-permute-start | bytes 393224 | tf_op jit(solution)/shard_map/ppermute | solution.py:352
  38.7 4.3 %collective-permute-start.11 = (bf16[2,256,128]{2,1,0:T(8,128)(2,1)S(1)}, bf16[2,256,128]{2,1,0:T(8,128)(2,1)S(1)}, u32[]{:S(2)}, u32[]{:S(2)}) collective-permute-start(bf16[2,256,128]{2,1,0:T(8,128)(2,1)S(1)} %collective-permute-done.9.refs_1_), channel_id=1, source_target_pairs={{0,1},{1,0},{2,3},{3,2},{4,5},{5,4},{6,7},{7,6},{8,9},{9,8},{10,11... | collective-permute-start | bytes 393224 | tf_op jit(solution)/shard_map/ppermute | solution.py:352
  42.9 2.1 %collective-permute-start.10 = (bf16[2,256,128]{2,1,0:T(8,128)(2,1)S(1)}, bf16[2,256,128]{2,1,0:T(8,128)(2,1)S(1)}, u32[]{:S(2)}, u32[]{:S(2)}) collective-permute-start(bf16[2,256,128]{2,1,0:T(8,128)(2,1)S(1)} %collective-permute-done.5.refs_1_), channel_id=1, source_target_pairs={{0,1},{1,0},{2,3},{3,2},{4,5},{5,4},{6,7},{7,6},{8,9},{9,8},{10,11... | collective-permute-start | bytes 393224 | tf_op jit(solution)/shard_map/ppermute | solution.py:352

commit v2 on v1

--- a/solution.py
+++ b/solution.py
@@ -56,16 +56,14 @@
     return pos + core * (n // 2)
 
 
-def pool_body(
-    n, me_ref, feat_hbm, occ_hbm, hgt_hbm, part_ref, xy_ref, xz_ref, feat_ref,
-    occ_ref, hgt_ref, by_z_ref, by_cell_ref, wide_ref, picks_ref, scale_ref, seen_ref, xz_acc, feat_sems,
-    side_sems,
+def partial_body(
+    n, me_ref, feat_hbm, occ_hbm, hgt_hbm, part_ref, by_z_ref, feat_ref,
+    occ_ref, hgt_ref, by_cell_ref, wide_ref, seen_ref, feat_sems, side_sems,
 ):
     rows, y_len, zs, chans = feat_ref.shape
     ys = y_len // n
     tiles, cells, _ = wide_ref.shape
     tile_y, lanes, stack = cells // zs, chans, rows * zs
-    both = tile_y + zs
 
     def fetch(t):
         at = pl.ds(t * tile_y, tile_y)
@@ -82,25 +80,18 @@
     iota = lambda shape, axis: lax.broadcasted_iota(jnp.int32, shape, axis)
     widen = (iota((stack, rows * chans), 0) // zs == iota((stack, rows * chans), 1) // chans).astype(F32).astype(BF)
     same_z = (iota((stack, cells), 0) % zs == iota((stack, cells), 1) % zs).astype(F32)
-    same_y = (iota((tile_y, cells), 0) == iota((tile_y, cells), 1) // zs).astype(F32)
     zidx = iota((zs, lanes), 0)
+    parts = lanes // tile_y
+    spread = (iota((lanes, parts * cells), 0) == iota((lanes, parts * cells), 1) // zs).astype(F32).astype(BF)
     for side in sides:
         side.wait()
 
-    parts = lanes // tile_y
-    spread = (iota((lanes, parts * cells), 0) == iota((lanes, parts * cells), 1) // zs).astype(F32).astype(BF)
-    xz_count = [0.0] * rows
     for block in range(y_len // lanes):
         at = slice(block * lanes, (block + 1) * lanes)
         weights = [
             jnp.where(zidx < hgt_ref[x : x + 1, at], occ_ref[x, :, at], 0).astype(F32) for x in range(rows)
         ]
         seen_ref[block] = sum(weights[1:], weights[0])
-        xy_count = [jnp.sum(w, axis=0, keepdims=True) for w in weights]
-        xy_count += [jnp.zeros((1, lanes), F32)] * (8 - rows % 8)
-        scale_ref[at, : len(xy_count)] = lax.rsqrt(1.0 + jnp.concatenate(xy_count, axis=0)).T
-        for x in range(rows):
-            xz_count[x] = xz_count[x] + jnp.sum(weights[x], axis=1, keepdims=True)
         stacked = jnp.concatenate(weights, axis=0).astype(BF)
         for part in range(parts):
             columns = slice(part * cells, (part + 1) * cells)
@@ -111,14 +102,7 @@
         by_cell_ref[t] = by_z_ref[t].T.astype(BF)
     for t in range(tiles):
         wide_ref[t] = jnp.dot(by_cell_ref[t], widen, preferred_element_type=F32)
-    for t in range(tiles):
-        picks = []
-        for x in range(rows):
-            row_z = by_z_ref[t, x * zs : (x + 1) * zs]
-            picks += [jnp.sum(row_z, axis=0, keepdims=True) * same_y, row_z]
-        picks_ref[t] = jnp.concatenate(picks, axis=0).astype(BF)
-
-    xz_acc[...] = jnp.zeros_like(xz_acc)
+
     group = min(ys, tile_y)
 
     def tile(t, _):
@@ -138,58 +122,93 @@
                 part_ref[home, pl.ds(at, zs), :] = total.astype(BF)
             shift = lax.rem(lanes - lax.rem(start - inner, lanes), lanes)
             part_ref[home, ys * zs :, :] = pltpu.roll(seen_ref[start // lanes], shift, 1).astype(BF)
+
+    lax.fori_loop(0, tiles, tile, None)
+
+
+def partials(feat, occ, hgt, me, n):
+    rows, y_len, zs, chans = feat.shape
+    ys = y_len // n
+    tile_y = 256 // zs
+    tiles, cells = y_len // tile_y, tile_y * zs
+    vmem = pl.BlockSpec(memory_space=pltpu.VMEM)
+    hbm = pl.BlockSpec(memory_space=pltpu.MemorySpace.HBM)
+    return pl.pallas_call(
+        functools.partial(partial_body, n),
+        in_specs=[pl.BlockSpec(memory_space=pltpu.SMEM), hbm, hbm, hbm],
+        out_specs=[vmem] * 3,
+        out_shape=[
+            jax.ShapeDtypeStruct((n, ys * zs + zs, chans), BF),
+            jax.ShapeDtypeStruct((tiles, rows * zs, cells), F32),
+            jax.ShapeDtypeStruct(feat.shape, BF),
+        ],
+        scratch_shapes=[
+            pltpu.VMEM(occ.shape, jnp.int32),
+            pltpu.VMEM(hgt.shape, jnp.int32),
+            pltpu.VMEM((tiles, cells, rows * zs), BF),
+            pltpu.VMEM((tiles, cells, rows * chans), F32),
+            pltpu.VMEM((y_len // chans, zs, chans), F32),
+            pltpu.SemaphoreType.DMA((tiles,)),
+            pltpu.SemaphoreType.DMA((2,)),
+        ],
+        compiler_params=pltpu.CompilerParams(vmem_limit_bytes=24 << 20),
+        cost_estimate=pl.CostEstimate(flops=8 * feat.size, bytes_accessed=2 * feat.size, transcendentals=0),
+        name="partials",
+    )(me.reshape(1), *(pltpu.with_memory_space_constraint(a, pltpu.MemorySpace.HBM) for a in (feat, occ, hgt)))
+
+
+def pool_body(feat_ref, by_z_ref, xy_ref, xz_ref, xz_acc, xz_cnt):
+    rows, _, zs, chans = feat_ref.shape
+    _, _, ys, _ = xy_ref.shape
+    tiles, _, cells = by_z_ref.shape
+    tile_y = cells // zs
+    both, group = tile_y + zs, min(ys, tile_y)
+    iota = lambda axis: lax.broadcasted_iota(jnp.int32, (tile_y, cells), axis)
+    same_y = (iota(0) == iota(1) // zs).astype(F32)
+    ones = jnp.ones((cells, chans), BF)
+    xz_acc[...] = jnp.zeros_like(xz_acc)
+    xz_cnt[...] = jnp.zeros_like(xz_cnt)
+
+    def tile(t, _):
+        first = t * tile_y
+        picks = []
+        for x in range(rows):
+            row_z = by_z_ref[t, x * zs : (x + 1) * zs]
+            picks += [jnp.sum(row_z, axis=0, keepdims=True) * same_y, row_z]
+        picks = jnp.concatenate(picks, axis=0).astype(BF)
+        counts = jnp.dot(picks, ones, preferred_element_type=F32)
         for x in range(rows):
             pick = slice(x * both, (x + 1) * both)
             cells_x = feat_ref[x, pl.ds(first, tile_y)].reshape(cells, chans)
-            sums = jnp.dot(picks_ref[t, pick], cells_x, preferred_element_type=F32)
-            scale = scale_ref[pl.ds(pl.multiple_of(first, tile_y), tile_y), x : x + 1]
-            pool = (sums[:tile_y] * jnp.broadcast_to(scale, (tile_y, chans))).astype(BF)
+            sums = jnp.dot(picks[pick], cells_x, preferred_element_type=F32)
+            pool = (sums[:tile_y] * lax.rsqrt(1.0 + counts[pick][:tile_y])).astype(BF)
             for g in range(tile_y // group):
                 start = first + g * group
                 at = slice(None) if group == ys else pl.ds(pl.multiple_of(start % ys, group), group)
                 xy_ref[start // ys, x, at] = pool[g * group : (g + 1) * group]
             xz_acc[x] += sums[tile_y:]
+            xz_cnt[x] += counts[pick][tile_y:]
 
     lax.fori_loop(0, tiles, tile, None)
-    for x in range(rows):
-        scale = lax.rsqrt(1.0 + jnp.broadcast_to(xz_count[x], (zs, chans)))
-        xz_ref[x] = (xz_acc[x] * scale).astype(BF)
-
-
-def pools(feat, occ, hgt, me, n):
+    xz_ref[...] = (xz_acc[...] * lax.rsqrt(1.0 + xz_cnt[...])).astype(BF)
+
+
+def pools(feat, by_z, n):
     rows, y_len, zs, chans = feat.shape
-    ys = y_len // n
-    tile_y = 256 // zs
-    tiles, cells = y_len // tile_y, tile_y * zs
-    vmem = pl.BlockSpec(memory_space=pltpu.VMEM)
-    hbm = pl.BlockSpec(memory_space=pltpu.MemorySpace.HBM)
+    vmem = pl.BlockSpec(memory_space=pltpu.VMEM)
     return pl.pallas_call(
-        functools.partial(pool_body, n),
-        in_specs=[pl.BlockSpec(memory_space=pltpu.SMEM), hbm, hbm, hbm],
-        out_specs=[vmem] * 4,
+        pool_body,
+        in_specs=[vmem] * 2,
+        out_specs=[vmem] * 2,
         out_shape=[
-            jax.ShapeDtypeStruct((n, ys * zs + zs, chans), BF),
-            jax.ShapeDtypeStruct((n, rows, ys, chans), BF),
+            jax.ShapeDtypeStruct((n, rows, y_len // n, chans), BF),
             jax.ShapeDtypeStruct((rows, zs, chans), BF),
-            jax.ShapeDtypeStruct(feat.shape, BF),
         ],
-        scratch_shapes=[
-            pltpu.VMEM(occ.shape, jnp.int32),
-            pltpu.VMEM(hgt.shape, jnp.int32),
-            pltpu.VMEM((tiles, rows * zs, cells), F32),
-            pltpu.VMEM((tiles, cells, rows * zs), BF),
-            pltpu.VMEM((tiles, cells, rows * chans), F32),
-            pltpu.VMEM((tiles, rows * (tile_y + zs), cells), BF),
-            pltpu.VMEM((y_len, 16), F32),
-            pltpu.VMEM((y_len // chans, zs, chans), F32),
-            pltpu.VMEM((rows, zs, chans), F32),
-            pltpu.SemaphoreType.DMA((tiles,)),
-            pltpu.SemaphoreType.DMA((2,)),
-        ],
-        compiler_params=pltpu.CompilerParams(vmem_limit_bytes=24 << 20),
-        cost_estimate=pl.CostEstimate(flops=8 * feat.size, bytes_accessed=2 * feat.size, transcendentals=0),
+        scratch_shapes=[pltpu.VMEM((rows, zs, chans), F32)] * 2,
+        compiler_params=pltpu.CompilerParams(vmem_limit_bytes=8 << 20),
+        cost_estimate=pl.CostEstimate(flops=2 * 32 * feat.size, bytes_accessed=1 << 20, transcendentals=0),
         name="pools",
-    )(me.reshape(1), *(pltpu.with_memory_space_constraint(a, pltpu.MemorySpace.HBM) for a in (feat, occ, hgt)))
+    )(feat, by_z)
 
 
 def planes_body(xy_ref, xz_ref, xy_in, xy_out, xz_in, xz_out, xy_plane, xz_plane):
@@ -355,12 +374,8 @@
 def per_device(n, features, occupancy, heights, xy_in, xy_out, xz_in, xz_out, yz_in, yz_out, voxel_in, voxel_out):
     zs = features.shape[2]
     me = lax.axis_index("gx")
-    parts, xy_pool, xz_pool, feat = pools(features, jnp.swapaxes(occupancy, 1, 2), heights, me, n)
+    parts, by_z, feat = partials(features, jnp.swapaxes(occupancy, 1, 2), heights, me, n)
     chans = features.shape[3]
-    xy_plane, xz_plane = planes(
-        xy_pool.reshape(-1, chans), xz_pool.reshape(-1, chans), xy_in, xy_out, xz_in, xz_out
-    )
-    first = first_layer(feat, xy_plane.reshape(xy_pool.shape), xz_plane.reshape(xz_pool.shape), voxel_in)
 
     digits = radices(n)
     weights = [1]
@@ -373,10 +388,18 @@
             swap(held[d * size : (d + 1) * size], n, mask(d, weights[stage])) for d in range(1, digit)
         ]
         if stage == 1:
-            pieces, first = lax.optimization_barrier((pieces, first))
+            pieces, xy_plane, xz_plane = lax.optimization_barrier((pieces, xy_plane, xz_plane))
         held = sum(piece.astype(F32) for piece in pieces).astype(BF)
+        if stage == 0:
+            held, by_z = lax.optimization_barrier((held, by_z))
+            xy_pool, xz_pool = pools(feat, by_z, n)
+            xy_plane, xz_plane = planes(
+                xy_pool.reshape(-1, chans), xz_pool.reshape(-1, chans), xy_in, xy_out, xz_in, xz_out
+            )
+    first = first_layer(feat, xy_plane.reshape(xy_pool.shape), xz_plane.reshape(xz_pool.shape), voxel_in)
     slower = digits[-1]
     pieces = [held] + [swap(held, n, mask(d, weights[len(digits) - 1])) for d in range(1, slower)]
+    pieces, first = lax.optimization_barrier((pieces, first))
     plane = yz_mlp(pieces, zs, yz_in, yz_out)
 
     call = functools.partial(voxels, me=me, shape=features.shape, first=first, w_in=voxel_in, w_out=voxel_out)

time: 47 us -> 45.3 us (0.964)
  waiting for transfers between devices: 10.5 us -> 6.94 us
  Pallas kernels: 23.4 us -> 25.2 us
    ppermute x12, waiting for transfers between devices: 10.5 us -> 6.94 us  [swap(): return lax.ppermute(value, 'gx', [(i, i ^ offset) for i in range(n)])]
    pallas_call x1 -> x2, Pallas kernels: 6.43 us -> 8.28 us  [the longest x1 4.77 us: partials(): pl.pallas_call(functools.partial(partial_body, n), in_specs=[pl.BlockSpec...]
  transfers between devices with their start and end apart: 12 -> 12, of which waited for: 5 -> 5; matrix products, arithmetic and copies ran while one was open for 0% -> 0% of each run, Pallas kernels for 31% -> 40%
where the time goes in v2:
time: 45.3 us; the launch traced here: 45.2 us
  Pallas kernels  25.2 us (56%)
  starting transfers between devices  12.5 us (28%)
  waiting for transfers between devices  6.94 us (15%)
    ppermute x12, starting transfers between devices, swap(): return lax.ppermute(value, 'gx', [(i, i ^ offset) for i in range(n)])  12.5 us
    pallas_call x6, Pallas kernels, voxels(): pl.pallas_call(functools.partial(voxel_body, n, groups, before, last), in...  8.97 us
    ppermute x12, waiting for transfers between devices, swap(): return lax.ppermute(value, 'gx', [(i, i ^ offset) for i in range(n)])  6.94 us
    pallas_call x1, Pallas kernels, first_layer(): pl.pallas_call(first_body, in_specs=[vmem] * 4, out_specs=vmem, out_shape...  5.8 us
    pallas_call x1, Pallas kernels, partials(): pl.pallas_call(functools.partial(partial_body, n), in_specs=[pl.BlockSpec...  4.77 us
    pallas_call x1, Pallas kernels, pools(): pl.pallas_call(pool_body, in_specs=[vmem] * 2, out_specs=[vmem] * 2, out_...  3.51 us
    pallas_call x1, Pallas kernels, planes(): pl.pallas_call(planes_body, in_specs=[vmem] * 6, out_specs=[vmem] * 2, ou...  1.63 us
  transfers between devices with their start and end apart: 12, of which 5 were waited for; matrix products, arithmetic and copies ran while one was open for 0% of the time, Pallas kernels for 40%

profile of v2, /device:TPU:0, one launch (start us, length us, event | category | flops | bytes accessed | tf_op | source)
XLA Modules:
  0.0 45.2 jit_solution(12649490634860266878)
XLA Ops:
  0.0 4.8 %partials.1 = (bf16[16,272,128]{2,1,0:T(8,128)(2,1)S(1)}, f32[16,96,256]{2,1,0:T(8,128)S(1)}, bf16[6,256,16,128]{3,2,1,0:T(8,128)(2,1)S(1)}) custom-call(s32[1]{0:T(128)} %bitcast.me_ref, bf16[6,256,16,128]{3,2,1,0:T(8,128)(2,1)} %feat_hbm.1, s32[6,16,256]{2,1,0:T(8,128)} %bitcast.10, s32[6,256]{1,0:T(8,128)} %hgt_hbm.1), custom_call_target="tpu_custom_call" | custom-call | flops 25165824 | bytes 6291456 | tf_op jit(solution)/shard_map/partials/pallas_call | solution.py:136
  4.8 0.0 copy-start.4
  4.8 0.0 copy-start.5
  4.8 0.0 copy-start.6
  4.8 0.0 copy-start.7
  4.9 0.0 copy-start
  4.9 0.6 %collective-permute-start = (bf16[8,272,128]{2,1,0:T(8,128)(2,1)S(1)}, bf16[8,272,128]{2,1,0:T(8,128)(2,1)S(1)}, u32[]{:S(2)}, u32[]{:S(2)}) collective-permute-start(bf16[8,272,128]{2,1,0:T(8,128)(2,1)S(1)} %slice.19), channel_id=1, source_target_pairs={{0,1},{1,0},{2,3},{3,2},{4,5},{5,4},{6,7},{7,6},{8,9},{9,8},{10,11... | collective-permute-start | bytes 1671176 | tf_op jit(solution)/shard_map/ppermute | solution.py:371
  5.4 1.6 %collective-permute-done = bf16[8,272,128]{2,1,0:T(8,128)(2,1)S(1)} collective-permute-done((bf16[8,272,128]{2,1,0:T(8,128)(2,1)S(1)}, bf16[8,272,128]{2,1,0:T(8,128)(2,1)S(1)}, u32[]{:S(2)}, u32[]{:S(2)}) %collective-permute-start) | collective-permute-done | bytes 557088 | tf_op jit(solution)/shard_map/ppermute | solution.py:371
  7.0 0.1 add_convert_fusion
  7.2 3.7 %collective-permute-start.3 = (bf16[2,272,128]{2,1,0:T(8,128)(2,1)S(1)}, bf16[2,272,128]{2,1,0:T(8,128)(2,1)S(1)}, u32[]{:S(2)}, u32[]{:S(2)}) collective-permute-start(bf16[2,272,128]{2,1,0:T(8,128)(2,1)S(1)} %get-tuple-element.79), channel_id=1, source_target_pairs={{0,7},{1,6},{2,5},{3,4},{4,3},{5,2},{6,1},{7,0},{8,15},{9,14},{10,... | collective-permute-start | bytes 417800 | tf_op jit(solution)/shard_map/ppermute | solution.py:371
  10.9 0.4 collective-permute-start.2
  11.4 0.2 collective-permute-start.1
  11.5 3.5 %pools.1 = (bf16[16,6,16,128]{3,2,1,0:T(8,128)(2,1)S(1)}, bf16[6,16,128]{2,1,0:T(8,128)(2,1)S(1)}) custom-call(bf16[6,256,16,128]{3,2,1,0:T(8,128)(2,1)S(1)} %get-tuple-element.45.feat_ref, f32[16,96,256]{2,1,0:T(8,128)S(1)} %get-tuple-element.46.by_z_ref), custom_call_target="tpu_custom_call" | custom-call | flops 201326592 | bytes 1048576 | tf_op jit(solution)/shard_map/pools/pallas_call | solution.py:199
  15.1 0.0 copy-done.4
  15.1 0.0 copy-done.5
  15.1 0.0 copy-done.6
  15.1 0.0 copy-done.7
  15.1 1.6 %planes.1 = (bf16[1536,128]{1,0:T(8,128)(2,1)S(1)}, bf16[96,128]{1,0:T(8,128)(2,1)S(1)}) custom-call(bf16[1536,128]{1,0:T(8,128)(2,1)S(1)} %bitcast.8, bf16[96,128]{1,0:T(8,128)(2,1)S(1)} %bitcast.9, bf16[128,512]{1,0:T(8,128)(2,1)S(1)} %copy-done.4, bf16[512,128]{1,0:T(8,128)(2,1)S(1)} %copy-done.5, bf16[128,512]{1,0:T(8,128)(2,1)S(1)} %copy-done.6, ...), custom_call_target="tpu_custom_call" | custom-call | flops 427819008 | bytes 1048576 | tf_op jit(solution)/shard_map/planes/pallas_call | solution.py:224
  16.7 0.0 collective-permute-done.3
  16.7 1.5 %collective-permute-done.2 = bf16[2,272,128]{2,1,0:T(8,128)(2,1)S(1)} collective-permute-done((bf16[2,272,128]{2,1,0:T(8,128)(2,1)S(1)}, bf16[2,272,128]{2,1,0:T(8,128)(2,1)S(1)}, u32[]{:S(2)}, u32[]{:S(2)}) %collective-permute-start.2) | collective-permute-done | bytes 139296 | tf_op jit(solution)/shard_map/ppermute | solution.py:371
  18.3 0.0 collective-permute-done.1
  18.3 0.1 add_convert_fusion.1.refs_0_
  18.4 2.8 %collective-permute-start.4 = (bf16[2,272,128]{2,1,0:T(8,128)(2,1)S(1)}, bf16[2,272,128]{2,1,0:T(8,128)(2,1)S(1)}, u32[]{:S(2)}, u32[]{:S(2)}) collective-permute-start(bf16[2,272,128]{2,1,0:T(8,128)(2,1)S(1)} %add_convert_fusion.1.refs_0_), channel_id=1, source_target_pairs={{0,8},{1,9},{2,10},{3,11},{4,12},{5,13},{6,14},{7,15},{8,0},{9,1},... | collective-permute-start | bytes 417800 | tf_op jit(solution)/shard_map/ppermute | solution.py:371
  21.2 5.8 %first_layer.1.first_ref = f32[16,6,256,256]{3,2,1,0:T(8,128)S(1)} custom-call(bf16[6,256,16,128]{3,2,1,0:T(8,128)(2,1)S(1)} %get-tuple-element.45.feat_ref, bf16[16,6,16,128]{3,2,1,0:T(8,128)(2,1)S(1)} %bitcast.6, bf16[6,16,128]{2,1,0:T(8,128)(2,1)S(1)} %bitcast.7, bf16[128,256]{1,0:T(8,128)(2,1)S(1)} %copy-done), custom_call_target="tpu_custom_call" | custom-call | flops 1610612736 | bytes 1048576 | tf_op jit(solution)/shard_map/first_layer/pallas_call | solution.py:287
  27.0 1.1 %collective-permute-done.4.refs_1_ = bf16[2,272,128]{2,1,0:T(8,128)(2,1)S(1)} collective-permute-done((bf16[2,272,128]{2,1,0:T(8,128)(2,1)S(1)}, bf16[2,272,128]{2,1,0:T(8,128)(2,1)S(1)}, u32[]{:S(2)}, u32[]{:S(2)}) %collective-permute-start.4) | collective-permute-done | bytes 139296 | tf_op jit(solution)/shard_map/ppermute | solution.py:371
  28.2 0.0 copy-done.2
  28.2 0.5 %yz_mlp.1.refs_0_ = bf16[2,256,128]{2,1,0:T(8,128)(2,1)S(1)} custom-call(bf16[2,272,128]{2,1,0:T(8,128)(2,1)S(1)} %add_convert_fusion.1.refs_0_, bf16[2,272,128]{2,1,0:T(8,128)(2,1)S(1)} %collective-permute-done.4.refs_1_, bf16[128,512]{1,0:T(8,128)(2,1)S(1)} %copy-done.2, bf16[512,128]{1,0:T(8,128)(2,1)S(1)} %copy-done.3), custom_call_target="tpu_custom_call" | custom-call | flops 134217728 | bytes 524288 | tf_op jit(solution)/shard_map/yz_mlp/pallas_call | solution.py:256
  28.7 0.1 collective-permute-start.7
  28.7 1.6 %collective-permute-start.6 = (bf16[2,256,128]{2,1,0:T(8,128)(2,1)S(1)}, bf16[2,256,128]{2,1,0:T(8,128)(2,1)S(1)}, u32[]{:S(2)}, u32[]{:S(2)}) collective-permute-start(bf16[2,256,128]{2,1,0:T(8,128)(2,1)S(1)} %yz_mlp.1.refs_0_), channel_id=1, source_target_pairs={{0,3},{1,2},{2,1},{3,0},{4,7},{5,6},{6,5},{7,4},{8,11},{9,10},{10,... | collective-permute-start | bytes 393224 | tf_op jit(solution)/shard_map/ppermute | solution.py:371
  30.4 0.4 collective-permute-start.9
  30.8 0.0 copy-done.1
  30.8 1.1 %voxels.6 = (bf16[6,256,16,128]{3,2,1,0:T(8,128)(2,1)}, bf16[2,6,16,16,128]{4,3,2,1,0:T(8,128)(2,1)S(1)}) custom-call(s32[1]{0:T(128)} %bitcast.me_ref, f32[16,6,256,256]{3,2,1,0:T(8,128)S(1)} %first_layer.1.first_ref, bf16[128,256]{1,0:T(8,128)(2,1)S(1)} %copy-done, bf16[256,128]{1,0:T(8,128)(2,1)S(1)} %copy-done.1, bf16[2,256,128]{2,1,0:T(8,128)(2,1)S(1)} %yz_mlp.1.refs_0_), custom_call_target="tpu_custom_call" | custom-call | flops 402653184 | bytes 1048576 | tf_op jit(solution)/shard_map/voxels/pallas_call | solution.py:351
  31.8 0.0 collective-permute-done.7.refs_0_
  31.8 1.1 %voxels.7 = (bf16[6,256,16,128]{3,2,1,0:T(8,128)(2,1)}, bf16[2,6,16,16,128]{4,3,2,1,0:T(8,128)(2,1)S(1)}) custom-call(s32[1]{0:T(128)} %bitcast.me_ref, f32[16,6,256,256]{3,2,1,0:T(8,128)S(1)} %first_layer.1.first_ref, bf16[128,256]{1,0:T(8,128)(2,1)S(1)} %copy-done, bf16[256,128]{1,0:T(8,128)(2,1)S(1)} %copy-done.1, ...), custom_call_target="tpu_custom_call", output_to_operand_aliasing={{0}: (6, {})} | custom-call | flops 402653184 | bytes 1048576 | tf_op jit(solution)/shard_map/voxels/pallas_call | solution.py:351
  32.9 1.1 %collective-permute-done.6.refs_0_ = bf16[2,256,128]{2,1,0:T(8,128)(2,1)S(1)} collective-permute-done((bf16[2,256,128]{2,1,0:T(8,128)(2,1)S(1)}, bf16[2,256,128]{2,1,0:T(8,128)(2,1)S(1)}, u32[]{:S(2)}, u32[]{:S(2)}) %collective-permute-start.6) | collective-permute-done | bytes 131104 | tf_op jit(solution)/shard_map/ppermute | solution.py:371
  34.0 0.7 %collective-permute-start.8 = (bf16[2,256,128]{2,1,0:T(8,128)(2,1)S(1)}, bf16[2,256,128]{2,1,0:T(8,128)(2,1)S(1)}, u32[]{:S(2)}, u32[]{:S(2)}) collective-permute-start(bf16[2,256,128]{2,1,0:T(8,128)(2,1)S(1)} %collective-permute-done.6.refs_0_), channel_id=1, source_target_pairs={{0,1},{1,0},{2,3},{3,2},{4,5},{5,4},{6,7},{7,6},{8,9},{9,8},{10,11... | collective-permute-start | bytes 393224 | tf_op jit(solution)/shard_map/ppermute | solution.py:371
  34.7 1.3 %collective-permute-start.5 = (bf16[2,256,128]{2,1,0:T(8,128)(2,1)S(1)}, bf16[2,256,128]{2,1,0:T(8,128)(2,1)S(1)}, u32[]{:S(2)}, u32[]{:S(2)}) collective-permute-start(bf16[2,256,128]{2,1,0:T(8,128)(2,1)S(1)} %yz_mlp.1.refs_0_), channel_id=1, source_target_pairs={{0,7},{1,6},{2,5},{3,4},{4,3},{5,2},{6,1},{7,0},{8,15},{9,14},{10,... | collective-permute-start | bytes 393224 | tf_op jit(solution)/shard_map/ppermute | solution.py:371
  36.0 1.1 %voxels.8 = (bf16[6,256,16,128]{3,2,1,0:T(8,128)(2,1)}, bf16[2,6,16,16,128]{4,3,2,1,0:T(8,128)(2,1)S(1)}) custom-call(s32[1]{0:T(128)} %bitcast.me_ref, f32[16,6,256,256]{3,2,1,0:T(8,128)S(1)} %first_layer.1.first_ref, bf16[128,256]{1,0:T(8,128)(2,1)S(1)} %copy-done, bf16[256,128]{1,0:T(8,128)(2,1)S(1)} %copy-done.1, ...), custom_call_target="tpu_custom_call", output_to_operand_aliasing={{0}: (6, {})} | custom-call | flops 402653184 | bytes 1048576 | tf_op jit(solution)/shard_map/voxels/pallas_call | solution.py:351
  37.1 0.0 collective-permute-done.9.refs_1_
  37.1 0.6 %collective-permute-start.11 = (bf16[2,256,128]{2,1,0:T(8,128)(2,1)S(1)}, bf16[2,256,128]{2,1,0:T(8,128)(2,1)S(1)}, u32[]{:S(2)}, u32[]{:S(2)}) collective-permute-start(bf16[2,256,128]{2,1,0:T(8,128)(2,1)S(1)} %collective-permute-done.9.refs_1_), channel_id=1, source_target_pairs={{0,1},{1,0},{2,3},{3,2},{4,5},{5,4},{6,7},{7,6},{8,9},{9,8},{10,11... | collective-permute-start | bytes 393224 | tf_op jit(solution)/shard_map/ppermute | solution.py:371
  37.7 0.0 collective-permute-done.8.refs_0_
  37.7 2.0 %voxels.9 = (bf16[6,256,16,128]{3,2,1,0:T(8,128)(2,1)}, bf16[4,6,16,16,128]{4,3,2,1,0:T(8,128)(2,1)S(1)}) custom-call(s32[1]{0:T(128)} %bitcast.me_ref, f32[16,6,256,256]{3,2,1,0:T(8,128)S(1)} %first_layer.1.first_ref, bf16[128,256]{1,0:T(8,128)(2,1)S(1)} %copy-done, bf16[256,128]{1,0:T(8,128)(2,1)S(1)} %copy-done.1, ...), custom_call_target="tpu_custom_call", output_to_operand_aliasing={{0}: (7, {})} | custom-call | flops 805306368 | bytes 1048576 | tf_op jit(solution)/shard_map/voxels/pallas_call | solution.py:351
  39.6 1.6 %collective-permute-done.5.refs_1_ = bf16[2,256,128]{2,1,0:T(8,128)(2,1)S(1)} collective-permute-done((bf16[2,256,128]{2,1,0:T(8,128)(2,1)S(1)}, bf16[2,256,128]{2,1,0:T(8,128)(2,1)S(1)}, u32[]{:S(2)}, u32[]{:S(2)}) %collective-permute-start.5) | collective-permute-done | bytes 131104 | tf_op jit(solution)/shard_map/ppermute | solution.py:371
  41.2 0.1 collective-permute-start.10
  41.3 0.0 collective-permute-done.11.refs_0_
  41.3 2.0 %voxels.10 = (bf16[6,256,16,128]{3,2,1,0:T(8,128)(2,1)}, bf16[4,6,16,16,128]{4,3,2,1,0:T(8,128)(2,1)S(1)}) custom-call(s32[1]{0:T(128)} %bitcast.me_ref, f32[16,6,256,256]{3,2,1,0:T(8,128)S(1)} %first_layer.1.first_ref, bf16[128,256]{1,0:T(8,128)(2,1)S(1)} %copy-done, bf16[256,128]{1,0:T(8,128)(2,1)S(1)} %copy-done.1, ...), custom_call_target="tpu_custom_call", output_to_operand_aliasing={{0}: (7, {})} | custom-call | flops 805306368 | bytes 1048576 | tf_op jit(solution)/shard_map/voxels/pallas_call | solution.py:351
  43.3 0.0 collective-permute-done.10.refs_0_
  43.3 1.8 %voxels.11 = bf16[6,256,16,128]{3,2,1,0:T(8,128)(2,1)} custom-call(s32[1]{0:T(128)} %bitcast.me_ref, f32[16,6,256,256]{3,2,1,0:T(8,128)S(1)} %first_layer.1.first_ref, bf16[128,256]{1,0:T(8,128)(2,1)S(1)} %copy-done, bf16[256,128]{1,0:T(8,128)(2,1)S(1)} %copy-done.1, ...), custom_call_target="tpu_custom_call", output_to_operand_aliasing={{}: (6, {})} | custom-call | flops 402653184 | bytes 1048576 | tf_op jit(solution)/shard_map/voxels/pallas_call | solution.py:351
  (7 shorter events, 0.1 us)
Async XLA Ops:
  4.8 10.3 %copy-start.4 = (bf16[128,512]{1,0:T(8,128)(2,1)S(1)}, bf16[128,512]{1,0:T(8,128)(2,1)}, u32[]{:S(2)}) copy-start(bf16[128,512]{1,0:T(8,128)(2,1)} %xy_in.1) | copy-start | bytes 393220
  4.8 10.3 %copy-start.5 = (bf16[512,128]{1,0:T(8,128)(2,1)S(1)}, bf16[512,128]{1,0:T(8,128)(2,1)}, u32[]{:S(2)}) copy-start(bf16[512,128]{1,0:T(8,128)(2,1)} %xy_out.1) | copy-start | bytes 393220
  4.8 10.3 %copy-start.6 = (bf16[128,512]{1,0:T(8,128)(2,1)S(1)}, bf16[128,512]{1,0:T(8,128)(2,1)}, u32[]{:S(2)}) copy-start(bf16[128,512]{1,0:T(8,128)(2,1)} %xz_in.1) | copy-start | bytes 393220
  4.8 10.3 %copy-start.7 = (bf16[512,128]{1,0:T(8,128)(2,1)S(1)}, bf16[512,128]{1,0:T(8,128)(2,1)}, u32[]{:S(2)}) copy-start(bf16[512,128]{1,0:T(8,128)(2,1)} %xz_out.1) | copy-start | bytes 393220
  4.9 16.3 %copy-start = (bf16[128,256]{1,0:T(8,128)(2,1)S(1)}, bf16[128,256]{1,0:T(8,128)(2,1)}, u32[]{:S(2)}) copy-start(bf16[128,256]{1,0:T(8,128)(2,1)} %w_in.13) | copy-start | bytes 196612
  4.9 2.1 %collective-permute-start = (bf16[8,272,128]{2,1,0:T(8,128)(2,1)S(1)}, bf16[8,272,128]{2,1,0:T(8,128)(2,1)S(1)}, u32[]{:S(2)}, u32[]{:S(2)}) collective-permute-start(bf16[8,272,128]{2,1,0:T(8,128)(2,1)S(1)} %slice.19), channel_id=1, source_target_pairs={{0,1},{1,0},{2,3},{3,2},{4,5},{5,4},{6,7},{7,6},{8,9},{9,8},{10,11... | collective-permute-start | bytes 1671176 | tf_op jit(solution)/shard_map/ppermute | solution.py:371
  7.2 9.5 %collective-permute-start.3 = (bf16[2,272,128]{2,1,0:T(8,128)(2,1)S(1)}, bf16[2,272,128]{2,1,0:T(8,128)(2,1)S(1)}, u32[]{:S(2)}, u32[]{:S(2)}) collective-permute-start(bf16[2,272,128]{2,1,0:T(8,128)(2,1)S(1)} %get-tuple-element.79), channel_id=1, source_target_pairs={{0,7},{1,6},{2,5},{3,4},{4,3},{5,2},{6,1},{7,0},{8,15},{9,14},{10,... | collective-permute-start | bytes 417800 | tf_op jit(solution)/shard_map/ppermute | solution.py:371
  10.9 7.4 %collective-permute-start.2 = (bf16[2,272,128]{2,1,0:T(8,128)(2,1)S(1)}, bf16[2,272,128]{2,1,0:T(8,128)(2,1)S(1)}, u32[]{:S(2)}, u32[]{:S(2)}) collective-permute-start(bf16[2,272,128]{2,1,0:T(8,128)(2,1)S(1)} %get-tuple-element.80), channel_id=1, source_target_pairs={{0,5},{1,4},{2,7},{3,6},{4,1},{5,0},{6,3},{7,2},{8,13},{9,12},{10,... | collective-permute-start | bytes 417800 | tf_op jit(solution)/shard_map/ppermute | solution.py:371
  11.4 6.9 %collective-permute-start.1 = (bf16[2,272,128]{2,1,0:T(8,128)(2,1)S(1)}, bf16[2,272,128]{2,1,0:T(8,128)(2,1)S(1)}, u32[]{:S(2)}, u32[]{:S(2)}) collective-permute-start(bf16[2,272,128]{2,1,0:T(8,128)(2,1)S(1)} %get-tuple-element.81), channel_id=1, source_target_pairs={{0,3},{1,2},{2,1},{3,0},{4,7},{5,6},{6,5},{7,4},{8,11},{9,10},{10,... | collective-permute-start | bytes 417800 | tf_op jit(solution)/shard_map/ppermute | solution.py:371
  18.4 9.8 %collective-permute-start.4 = (bf16[2,272,128]{2,1,0:T(8,128)(2,1)S(1)}, bf16[2,272,128]{2,1,0:T(8,128)(2,1)S(1)}, u32[]{:S(2)}, u32[]{:S(2)}) collective-permute-start(bf16[2,272,128]{2,1,0:T(8,128)(2,1)S(1)} %add_convert_fusion.1.refs_0_), channel_id=1, source_target_pairs={{0,8},{1,9},{2,10},{3,11},{4,12},{5,13},{6,14},{7,15},{8,0},{9,1},... | collective-permute-start | bytes 417800 | tf_op jit(solution)/shard_map/ppermute | solution.py:371
  21.2 6.9 %copy-start.2 = (bf16[128,512]{1,0:T(8,128)(2,1)S(1)}, bf16[128,512]{1,0:T(8,128)(2,1)}, u32[]{:S(2)}) copy-start(bf16[128,512]{1,0:T(8,128)(2,1)} %refs_2_.1) | copy-start | bytes 393220
  21.2 6.9 %copy-start.3 = (bf16[512,128]{1,0:T(8,128)(2,1)S(1)}, bf16[512,128]{1,0:T(8,128)(2,1)}, u32[]{:S(2)}) copy-start(bf16[512,128]{1,0:T(8,128)(2,1)} %refs_3_.1) | copy-start | bytes 393220
  21.2 9.6 %copy-start.1 = (bf16[256,128]{1,0:T(8,128)(2,1)S(1)}, bf16[256,128]{1,0:T(8,128)(2,1)}, u32[]{:S(2)}) copy-start(bf16[256,128]{1,0:T(8,128)(2,1)} %w_out.11) | copy-start | bytes 196612
  28.7 3.2 %collective-permute-start.7 = (bf16[2,256,128]{2,1,0:T(8,128)(2,1)S(1)}, bf16[2,256,128]{2,1,0:T(8,128)(2,1)S(1)}, u32[]{:S(2)}, u32[]{:S(2)}) collective-permute-start(bf16[2,256,128]{2,1,0:T(8,128)(2,1)S(1)} %yz_mlp.1.refs_0_), channel_id=1, source_target_pairs={{0,1},{1,0},{2,3},{3,2},{4,5},{5,4},{6,7},{7,6},{8,9},{9,8},{10,11... | collective-permute-start | bytes 393224 | tf_op jit(solution)/shard_map/ppermute | solution.py:371
  28.7 5.2 %collective-permute-start.6 = (bf16[2,256,128]{2,1,0:T(8,128)(2,1)S(1)}, bf16[2,256,128]{2,1,0:T(8,128)(2,1)S(1)}, u32[]{:S(2)}, u32[]{:S(2)}) collective-permute-start(bf16[2,256,128]{2,1,0:T(8,128)(2,1)S(1)} %yz_mlp.1.refs_0_), channel_id=1, source_target_pairs={{0,3},{1,2},{2,1},{3,0},{4,7},{5,6},{6,5},{7,4},{8,11},{9,10},{10,... | collective-permute-start | bytes 393224 | tf_op jit(solution)/shard_map/ppermute | solution.py:371
  30.4 6.7 %collective-permute-start.9 = (bf16[2,256,128]{2,1,0:T(8,128)(2,1)S(1)}, bf16[2,256,128]{2,1,0:T(8,128)(2,1)S(1)}, u32[]{:S(2)}, u32[]{:S(2)}) collective-permute-start(bf16[2,256,128]{2,1,0:T(8,128)(2,1)S(1)} %yz_mlp.1.refs_0_), channel_id=1, source_target_pairs={{0,5},{1,4},{2,7},{3,6},{4,1},{5,0},{6,3},{7,2},{8,13},{9,12},{10,... | collective-permute-start | bytes 393224 | tf_op jit(solution)/shard_map/ppermute | solution.py:371
  34.0 3.7 %collective-permute-start.8 = (bf16[2,256,128]{2,1,0:T(8,128)(2,1)S(1)}, bf16[2,256,128]{2,1,0:T(8,128)(2,1)S(1)}, u32[]{:S(2)}, u32[]{:S(2)}) collective-permute-start(bf16[2,256,128]{2,1,0:T(8,128)(2,1)S(1)} %collective-permute-done.6.refs_0_), channel_id=1, source_target_pairs={{0,1},{1,0},{2,3},{3,2},{4,5},{5,4},{6,7},{7,6},{8,9},{9,8},{10,11... | collective-permute-start | bytes 393224 | tf_op jit(solution)/shard_map/ppermute | solution.py:371
  34.7 6.5 %collective-permute-start.5 = (bf16[2,256,128]{2,1,0:T(8,128)(2,1)S(1)}, bf16[2,256,128]{2,1,0:T(8,128)(2,1)S(1)}, u32[]{:S(2)}, u32[]{:S(2)}) collective-permute-start(bf16[2,256,128]{2,1,0:T(8,128)(2,1)S(1)} %yz_mlp.1.refs_0_), channel_id=1, source_target_pairs={{0,7},{1,6},{2,5},{3,4},{4,3},{5,2},{6,1},{7,0},{8,15},{9,14},{10,... | collective-permute-start | bytes 393224 | tf_op jit(solution)/shard_map/ppermute | solution.py:371
  37.1 4.3 %collective-permute-start.11 = (bf16[2,256,128]{2,1,0:T(8,128)(2,1)S(1)}, bf16[2,256,128]{2,1,0:T(8,128)(2,1)S(1)}, u32[]{:S(2)}, u32[]{:S(2)}) collective-permute-start(bf16[2,256,128]{2,1,0:T(8,128)(2,1)S(1)} %collective-permute-done.9.refs_1_), channel_id=1, source_target_pairs={{0,1},{1,0},{2,3},{3,2},{4,5},{5,4},{6,7},{7,6},{8,9},{9,8},{10,11... | collective-permute-start | bytes 393224 | tf_op jit(solution)/shard_map/ppermute | solution.py:371
  41.2 2.1 %collective-permute-start.10 = (bf16[2,256,128]{2,1,0:T(8,128)(2,1)S(1)}, bf16[2,256,128]{2,1,0:T(8,128)(2,1)S(1)}, u32[]{:S(2)}, u32[]{:S(2)}) collective-permute-start(bf16[2,256,128]{2,1,0:T(8,128)(2,1)S(1)} %collective-permute-done.5.refs_1_), channel_id=1, source_target_pairs={{0,1},{1,0},{2,3},{3,2},{4,5},{5,4},{6,7},{7,6},{8,9},{9,8},{10,11... | collective-permute-start | bytes 393224 | tf_op jit(solution)/shard_map/ppermute | solution.py:371

commit v3 on v2

--- a/solution.py
+++ b/solution.py
@@ -56,18 +56,67 @@
     return pos + core * (n // 2)
 
 
+def sum_tiles(n, split, pos0, me, feat_ref, by_cell_ref, seen_ref, part_ref, even_ref, odd_ref, wait):
+    rows, y_len, zs, chans = feat_ref.shape
+    ys = y_len // n
+    tiles, cells, stack = by_cell_ref.shape
+    tile_y, lanes = cells // zs, chans
+    group = min(ys, tile_y)
+    steps = part_ref.shape[0] if split else tiles
+    iota = lambda axis: lax.broadcasted_iota(jnp.int32, (stack, rows * chans), axis)
+    widen = (iota(0) // zs == iota(1) // chans).astype(F32).astype(BF)
+
+    def tile_of(i):
+        return offset(pos0 + i, n) ^ me if split else i
+
+    def expand(i, wide_ref):
+        wide_ref[...] = jnp.dot(by_cell_ref[tile_of(i)], widen, preferred_element_type=F32)
+
+    def tile(i, wide_ref):
+        first = tile_of(i) * tile_y
+        for g in range(tile_y // group):
+            start = first + g * group
+            home, inner = i if split else position((start // ys) ^ me, n), start % ys
+            for y in range(group):
+                cell = (g * group + y) * zs
+                total = None
+                for x in range(rows):
+                    weight = wide_ref[cell : cell + zs, x * chans : (x + 1) * chans]
+                    term = feat_ref[x, start + y].astype(F32) * weight
+                    total = term if total is None else total + term
+                at = y * zs if group == ys else pl.multiple_of((inner + y) * zs, zs)
+                part_ref[home, pl.ds(at, zs), :] = total.astype(BF)
+            shift = lax.rem(lanes - lax.rem(start - inner, lanes), lanes)
+            part_ref[home, ys * zs :, :] = pltpu.roll(seen_ref[start // lanes], shift, 1).astype(BF)
+
+    def pair(p, _):
+        i = 2 * p
+        wait(tile_of(i))
+        wait(tile_of(i + 1))
+        expand(i + 1, odd_ref)
+        tile(i, even_ref)
+        expand(jnp.minimum(i + 2, steps - 1), even_ref)
+        tile(i + 1, odd_ref)
+
+    expand(0, even_ref)
+    lax.fori_loop(0, steps // 2, pair, None)
+
+
 def partial_body(
-    n, me_ref, feat_hbm, occ_hbm, hgt_hbm, part_ref, by_z_ref, feat_ref,
-    occ_ref, hgt_ref, by_cell_ref, wide_ref, seen_ref, feat_sems, side_sems,
+    n, split, me_ref, feat_hbm, occ_hbm, hgt_hbm, part_ref, by_z_ref, feat_ref, by_cell_ref, seen_ref,
+    occ_ref, hgt_ref, even_ref, odd_ref, feat_sems, side_sems,
 ):
     rows, y_len, zs, chans = feat_ref.shape
-    ys = y_len // n
-    tiles, cells, _ = wide_ref.shape
+    tiles, cells, _ = by_cell_ref.shape
     tile_y, lanes, stack = cells // zs, chans, rows * zs
+    me = me_ref[0]
 
     def fetch(t):
         at = pl.ds(t * tile_y, tile_y)
         return pltpu.make_async_copy(feat_hbm.at[:, at], feat_ref.at[:, at], feat_sems.at[t])
+
+    def tile_of(i):
+        return offset((i + tiles // 2) % tiles, n) ^ me if split else i
 
     sides = [
         pltpu.make_async_copy(occ_hbm, occ_ref, side_sems.at[0]),
@@ -75,10 +124,9 @@
     ]
     for side in sides:
         side.start()
-    lax.fori_loop(0, tiles, lambda t, _: fetch(t).start(), None)
+    lax.fori_loop(0, tiles, lambda i, _: fetch(tile_of(i)).start(), None)
 
     iota = lambda shape, axis: lax.broadcasted_iota(jnp.int32, shape, axis)
-    widen = (iota((stack, rows * chans), 0) // zs == iota((stack, rows * chans), 1) // chans).astype(F32).astype(BF)
     same_z = (iota((stack, cells), 0) % zs == iota((stack, cells), 1) % zs).astype(F32)
     zidx = iota((zs, lanes), 0)
     parts = lanes // tile_y
@@ -100,30 +148,17 @@
             )
     for t in range(tiles):
         by_cell_ref[t] = by_z_ref[t].T.astype(BF)
-    for t in range(tiles):
-        wide_ref[t] = jnp.dot(by_cell_ref[t], widen, preferred_element_type=F32)
-
-    group = min(ys, tile_y)
-
-    def tile(t, _):
-        first = t * tile_y
-        fetch(t).wait()
-        for g in range(tile_y // group):
-            start = first + g * group
-            home, inner = position((start // ys) ^ me_ref[0], n), start % ys
-            for y in range(group):
-                cell = (g * group + y) * zs
-                total = None
-                for x in range(rows):
-                    weight = wide_ref[t, cell : cell + zs, x * chans : (x + 1) * chans]
-                    term = feat_ref[x, start + y].astype(F32) * weight
-                    total = term if total is None else total + term
-                at = y * zs if group == ys else pl.multiple_of((inner + y) * zs, zs)
-                part_ref[home, pl.ds(at, zs), :] = total.astype(BF)
-            shift = lax.rem(lanes - lax.rem(start - inner, lanes), lanes)
-            part_ref[home, ys * zs :, :] = pltpu.roll(seen_ref[start // lanes], shift, 1).astype(BF)
-
-    lax.fori_loop(0, tiles, tile, None)
+    sum_tiles(
+        n, split, n // 2, me, feat_ref, by_cell_ref, seen_ref, part_ref, even_ref, odd_ref, lambda t: fetch(t).wait()
+    )
+    if split:
+        lax.fori_loop(tiles // 2, tiles, lambda i, _: fetch(tile_of(i)).wait(), None)
+
+
+def own_body(n, me_ref, feat_ref, by_cell_ref, seen_ref, part_ref, even_ref, odd_ref):
+    sum_tiles(
+        n, True, 0, me_ref[0], feat_ref, by_cell_ref, seen_ref, part_ref, even_ref, odd_ref, lambda t: None
+    )
 
 
 def partials(feat, occ, hgt, me, n):
@@ -131,30 +166,44 @@
     ys = y_len // n
     tile_y = 256 // zs
     tiles, cells = y_len // tile_y, tile_y * zs
+    split = ys == tile_y
     vmem = pl.BlockSpec(memory_space=pltpu.VMEM)
     hbm = pl.BlockSpec(memory_space=pltpu.MemorySpace.HBM)
-    return pl.pallas_call(
-        functools.partial(partial_body, n),
-        in_specs=[pl.BlockSpec(memory_space=pltpu.SMEM), hbm, hbm, hbm],
-        out_specs=[vmem] * 3,
+    smem = pl.BlockSpec(memory_space=pltpu.SMEM)
+    block = jax.ShapeDtypeStruct((n // 2 if split else n, ys * zs + zs, chans), BF)
+    wide = [pltpu.VMEM((cells, rows * chans), F32)] * 2
+    cost = pl.CostEstimate(flops=4 * feat.size, bytes_accessed=feat.size, transcendentals=0)
+    part, by_z, kept, by_cell, seen = pl.pallas_call(
+        functools.partial(partial_body, n, split),
+        in_specs=[smem, hbm, hbm, hbm],
+        out_specs=[vmem] * 5,
         out_shape=[
-            jax.ShapeDtypeStruct((n, ys * zs + zs, chans), BF),
+            block,
             jax.ShapeDtypeStruct((tiles, rows * zs, cells), F32),
             jax.ShapeDtypeStruct(feat.shape, BF),
+            jax.ShapeDtypeStruct((tiles, cells, rows * zs), BF),
+            jax.ShapeDtypeStruct((y_len // chans, zs, chans), F32),
         ],
-        scratch_shapes=[
-            pltpu.VMEM(occ.shape, jnp.int32),
-            pltpu.VMEM(hgt.shape, jnp.int32),
-            pltpu.VMEM((tiles, cells, rows * zs), BF),
-            pltpu.VMEM((tiles, cells, rows * chans), F32),
-            pltpu.VMEM((y_len // chans, zs, chans), F32),
-            pltpu.SemaphoreType.DMA((tiles,)),
-            pltpu.SemaphoreType.DMA((2,)),
-        ],
-        compiler_params=pltpu.CompilerParams(vmem_limit_bytes=24 << 20),
-        cost_estimate=pl.CostEstimate(flops=8 * feat.size, bytes_accessed=2 * feat.size, transcendentals=0),
+        scratch_shapes=[pltpu.VMEM(occ.shape, jnp.int32), pltpu.VMEM(hgt.shape, jnp.int32)]
+        + wide
+        + [pltpu.SemaphoreType.DMA((tiles,)), pltpu.SemaphoreType.DMA((2,))],
+        compiler_params=pltpu.CompilerParams(vmem_limit_bytes=16 << 20),
+        cost_estimate=cost,
         name="partials",
     )(me.reshape(1), *(pltpu.with_memory_space_constraint(a, pltpu.MemorySpace.HBM) for a in (feat, occ, hgt)))
+    if not split:
+        return part[n // 2 :], part[: n // 2], by_z, kept
+    own = pl.pallas_call(
+        functools.partial(own_body, n),
+        in_specs=[smem] + [vmem] * 3,
+        out_specs=vmem,
+        out_shape=block,
+        scratch_shapes=wide,
+        compiler_params=pltpu.CompilerParams(vmem_limit_bytes=8 << 20),
+        cost_estimate=cost,
+        name="own_partials",
+    )(me.reshape(1), kept, by_cell, seen)
+    return part, own, by_z, kept
 
 
 def pool_body(feat_ref, by_z_ref, xy_ref, xz_ref, xz_acc, xz_cnt):
@@ -374,19 +423,21 @@
 def per_device(n, features, occupancy, heights, xy_in, xy_out, xz_in, xz_out, yz_in, yz_out, voxel_in, voxel_out):
     zs = features.shape[2]
     me = lax.axis_index("gx")
-    parts, by_z, feat = partials(features, jnp.swapaxes(occupancy, 1, 2), heights, me, n)
+    theirs, held, by_z, feat = partials(features, jnp.swapaxes(occupancy, 1, 2), heights, me, n)
     chans = features.shape[3]
 
     digits = radices(n)
     weights = [1]
     for digit in digits:
         weights.append(weights[-1] * digit)
-    held = parts
     for stage, digit in enumerate(digits[:-1]):
         size = held.shape[0] // digit
-        pieces = [held[:size]] + [
-            swap(held[d * size : (d + 1) * size], n, mask(d, weights[stage])) for d in range(1, digit)
-        ]
+        if stage == 0:
+            pieces = [held, swap(theirs, n, 1)]
+        else:
+            pieces = [held[:size]] + [
+                swap(held[d * size : (d + 1) * size], n, mask(d, weights[stage])) for d in range(1, digit)
+            ]
         if stage == 1:
             pieces, xy_plane, xz_plane = lax.optimization_barrier((pieces, xy_plane, xz_plane))
         held = sum(piece.astype(F32) for piece in pieces).astype(BF)

time: 45.3 us -> 44.1 us (0.974)
  waiting for transfers between devices: 6.94 us -> 5.34 us
  Pallas kernels: 25.2 us -> 25.8 us
    ppermute x12, waiting for transfers between devices: 6.94 us -> 5.34 us  [swap(): return lax.ppermute(value, 'gx', [(i, i ^ offset) for i in range(n)])]
    pallas_call x1 -> x2, Pallas kernels: 4.77 us -> 5.32 us  [the longest x1 3.62 us: partials(): pl.pallas_call(functools.partial(partial_body, n, split), in_specs=[smem,...]
  transfers between devices with their start and end apart: 12 -> 12, of which waited for: 5 -> 5; matrix products, arithmetic and copies ran while one was open for 0% -> 0% of each run, Pallas kernels for 40% -> 45%
where the time goes in v3:
time: 44.1 us; the launch traced here: 43.9 us
  Pallas kernels  25.8 us (59%)
  starting transfers between devices  12.3 us (28%)
  waiting for transfers between devices  5.34 us (12%)
    ppermute x12, starting transfers between devices, swap(): return lax.ppermute(value, 'gx', [(i, i ^ offset) for i in range(n)])  12.3 us
    pallas_call x6, Pallas kernels, voxels(): pl.pallas_call(functools.partial(voxel_body, n, groups, before, last), in...  8.98 us
    pallas_call x1, Pallas kernels, first_layer(): pl.pallas_call(first_body, in_specs=[vmem] * 4, out_specs=vmem, out_shape...  5.79 us
    ppermute x12, waiting for transfers between devices, swap(): return lax.ppermute(value, 'gx', [(i, i ^ offset) for i in range(n)])  5.34 us
    pallas_call x1, Pallas kernels, partials(): pl.pallas_call(functools.partial(partial_body, n, split), in_specs=[smem,...  3.62 us
    pallas_call x1, Pallas kernels, pools(): pl.pallas_call(pool_body, in_specs=[vmem] * 2, out_specs=[vmem] * 2, out_...  3.51 us
    pallas_call x1, Pallas kernels, partials(): pl.pallas_call(functools.partial(own_body, n), in_specs=[smem] + [vmem] *...  1.71 us
    pallas_call x1, Pallas kernels, planes(): pl.pallas_call(planes_body, in_specs=[vmem] * 6, out_specs=[vmem] * 2, ou...  1.67 us
  transfers between devices with their start and end apart: 12, of which 5 were waited for; matrix products, arithmetic and copies ran while one was open for 0% of the time, Pallas kernels for 45%

profile of v3, /device:TPU:0, one launch (start us, length us, event | category | flops | bytes accessed | tf_op | source)
XLA Modules:
  0.0 43.9 jit_solution(9254233655098159389)
XLA Ops:
  0.0 3.6 %partials.1 = (bf16[8,272,128]{2,1,0:T(8,128)(2,1)S(1)}, f32[16,96,256]{2,1,0:T(8,128)S(1)}, bf16[6,256,16,128]{3,2,1,0:T(8,128)(2,1)S(1)}, bf16[16,256,96]{2,1,0:T(8,128)(2,1)S(1)}, f32[2,16,128]{2,1,0:T(8,128)S(1)}) custom-call(s32[1]{0:T(128)} %bitcast.me_ref, bf16[6,256,16,128]{3,2,1,0:T(8,128)(2,1)} %feat_hbm.1, s32[6,16,256]{2,1,0:T(8,128)} %bitcast.10, ...), custom_call_target="tpu_custom_call" | custom-call | flops 12582912 | bytes 3145728 | tf_op jit(solution)/shard_map/partials/pallas_call | solution.py:176
  3.6 0.6 %collective-permute-start = (bf16[8,272,128]{2,1,0:T(8,128)(2,1)S(1)}, bf16[8,272,128]{2,1,0:T(8,128)(2,1)S(1)}, u32[]{:S(2)}, u32[]{:S(2)}) collective-permute-start(bf16[8,272,128]{2,1,0:T(8,128)(2,1)S(1)} %get-tuple-element.47), channel_id=1, source_target_pairs={{0,1},{1,0},{2,3},{3,2},{4,5},{5,4},{6,7},{7,6},{8,9},{9,8},{10,11... | collective-permute-start | bytes 1671176 | tf_op jit(solution)/shard_map/ppermute | solution.py:420
  4.2 1.7 %own_partials.1 = bf16[8,272,128]{2,1,0:T(8,128)(2,1)S(1)} custom-call(s32[1]{0:T(128)} %bitcast.me_ref, bf16[6,256,16,128]{3,2,1,0:T(8,128)(2,1)S(1)} %get-tuple-element.44.feat_ref, bf16[16,256,96]{2,1,0:T(8,128)(2,1)S(1)} %get-tuple-element.45.by_cell_ref, f32[2,16,128]{2,1,0:T(8,128)S(1)} %get-tuple-element.46.seen_ref), custom_call_target="tpu_custom_call" | custom-call | flops 12582912 | bytes 3145728 | tf_op jit(solution)/shard_map/own_partials/pallas_call | solution.py:196
  5.9 0.0 copy-start.4
  5.9 0.0 copy-start.5
  5.9 0.0 copy-start.6
  5.9 0.0 copy-start.7
  5.9 0.0 copy-start
  6.0 0.0 collective-permute-done
  6.0 0.2 add_convert_fusion
  6.2 3.7 %collective-permute-start.3 = (bf16[2,272,128]{2,1,0:T(8,128)(2,1)S(1)}, bf16[2,272,128]{2,1,0:T(8,128)(2,1)S(1)}, u32[]{:S(2)}, u32[]{:S(2)}) collective-permute-start(bf16[2,272,128]{2,1,0:T(8,128)(2,1)S(1)} %get-tuple-element.83), channel_id=1, source_target_pairs={{0,7},{1,6},{2,5},{3,4},{4,3},{5,2},{6,1},{7,0},{8,15},{9,14},{10,... | collective-permute-start | bytes 417800 | tf_op jit(solution)/shard_map/ppermute | solution.py:420
  9.9 0.2 collective-permute-start.2
  10.1 0.2 collective-permute-start.1
  10.3 3.5 %pools.1 = (bf16[16,6,16,128]{3,2,1,0:T(8,128)(2,1)S(1)}, bf16[6,16,128]{2,1,0:T(8,128)(2,1)S(1)}) custom-call(bf16[6,256,16,128]{3,2,1,0:T(8,128)(2,1)S(1)} %get-tuple-element.44.feat_ref, f32[16,96,256]{2,1,0:T(8,128)S(1)} %get-tuple-element.50.by_z_ref), custom_call_target="tpu_custom_call" | custom-call | flops 201326592 | bytes 1048576 | tf_op jit(solution)/shard_map/pools/pallas_call | solution.py:248
  13.8 0.0 copy-done.4
  13.8 0.0 copy-done.5
  13.8 0.0 copy-done.6
  13.8 1.7 %planes.1 = (bf16[1536,128]{1,0:T(8,128)(2,1)S(1)}, bf16[96,128]{1,0:T(8,128)(2,1)S(1)}) custom-call(bf16[1536,128]{1,0:T(8,128)(2,1)S(1)} %bitcast.8, bf16[96,128]{1,0:T(8,128)(2,1)S(1)} %bitcast.9, bf16[128,512]{1,0:T(8,128)(2,1)S(1)} %copy-done.4, bf16[512,128]{1,0:T(8,128)(2,1)S(1)} %copy-done.5, bf16[128,512]{1,0:T(8,128)(2,1)S(1)} %copy-done.6, ...), custom_call_target="tpu_custom_call" | custom-call | flops 427819008 | bytes 1048576 | tf_op jit(solution)/shard_map/planes/pallas_call | solution.py:273
  15.5 0.0 collective-permute-done.3
  15.5 1.3 %collective-permute-done.2 = bf16[2,272,128]{2,1,0:T(8,128)(2,1)S(1)} collective-permute-done((bf16[2,272,128]{2,1,0:T(8,128)(2,1)S(1)}, bf16[2,272,128]{2,1,0:T(8,128)(2,1)S(1)}, u32[]{:S(2)}, u32[]{:S(2)}) %collective-permute-start.2) | collective-permute-done | bytes 139296 | tf_op jit(solution)/shard_map/ppermute | solution.py:420
  16.8 0.2 collective-permute-done.1
  17.0 0.1 add_convert_fusion.1.refs_0_
  17.1 2.8 %collective-permute-start.4 = (bf16[2,272,128]{2,1,0:T(8,128)(2,1)S(1)}, bf16[2,272,128]{2,1,0:T(8,128)(2,1)S(1)}, u32[]{:S(2)}, u32[]{:S(2)}) collective-permute-start(bf16[2,272,128]{2,1,0:T(8,128)(2,1)S(1)} %add_convert_fusion.1.refs_0_), channel_id=1, source_target_pairs={{0,8},{1,9},{2,10},{3,11},{4,12},{5,13},{6,14},{7,15},{8,0},{9,1},... | collective-permute-start | bytes 417800 | tf_op jit(solution)/shard_map/ppermute | solution.py:420
  19.9 5.8 %first_layer.1.first_ref = f32[16,6,256,256]{3,2,1,0:T(8,128)S(1)} custom-call(bf16[6,256,16,128]{3,2,1,0:T(8,128)(2,1)S(1)} %get-tuple-element.44.feat_ref, bf16[16,6,16,128]{3,2,1,0:T(8,128)(2,1)S(1)} %bitcast.6, bf16[6,16,128]{2,1,0:T(8,128)(2,1)S(1)} %bitcast.7, bf16[128,256]{1,0:T(8,128)(2,1)S(1)} %copy-done), custom_call_target="tpu_custom_call" | custom-call | flops 1610612736 | bytes 1048576 | tf_op jit(solution)/shard_map/first_layer/pallas_call | solution.py:336
  25.7 1.1 %collective-permute-done.4.refs_1_ = bf16[2,272,128]{2,1,0:T(8,128)(2,1)S(1)} collective-permute-done((bf16[2,272,128]{2,1,0:T(8,128)(2,1)S(1)}, bf16[2,272,128]{2,1,0:T(8,128)(2,1)S(1)}, u32[]{:S(2)}, u32[]{:S(2)}) %collective-permute-start.4) | collective-permute-done | bytes 139296 | tf_op jit(solution)/shard_map/ppermute | solution.py:420
  26.9 0.0 copy-done.3
  26.9 0.5 %yz_mlp.1.refs_0_ = bf16[2,256,128]{2,1,0:T(8,128)(2,1)S(1)} custom-call(bf16[2,272,128]{2,1,0:T(8,128)(2,1)S(1)} %add_convert_fusion.1.refs_0_, bf16[2,272,128]{2,1,0:T(8,128)(2,1)S(1)} %collective-permute-done.4.refs_1_, bf16[128,512]{1,0:T(8,128)(2,1)S(1)} %copy-done.2, bf16[512,128]{1,0:T(8,128)(2,1)S(1)} %copy-done.3), custom_call_target="tpu_custom_call" | custom-call | flops 134217728 | bytes 524288 | tf_op jit(solution)/shard_map/yz_mlp/pallas_call | solution.py:305
  27.4 0.1 collective-permute-start.7
  27.5 1.7 %collective-permute-start.6 = (bf16[2,256,128]{2,1,0:T(8,128)(2,1)S(1)}, bf16[2,256,128]{2,1,0:T(8,128)(2,1)S(1)}, u32[]{:S(2)}, u32[]{:S(2)}) collective-permute-start(bf16[2,256,128]{2,1,0:T(8,128)(2,1)S(1)} %yz_mlp.1.refs_0_), channel_id=1, source_target_pairs={{0,3},{1,2},{2,1},{3,0},{4,7},{5,6},{6,5},{7,4},{8,11},{9,10},{10,... | collective-permute-start | bytes 393224 | tf_op jit(solution)/shard_map/ppermute | solution.py:420
  29.1 0.3 collective-permute-start.9
  29.5 0.0 copy-done.1
  29.5 1.1 %voxels.6 = (bf16[6,256,16,128]{3,2,1,0:T(8,128)(2,1)}, bf16[2,6,16,16,128]{4,3,2,1,0:T(8,128)(2,1)S(1)}) custom-call(s32[1]{0:T(128)} %bitcast.me_ref, f32[16,6,256,256]{3,2,1,0:T(8,128)S(1)} %first_layer.1.first_ref, bf16[128,256]{1,0:T(8,128)(2,1)S(1)} %copy-done, bf16[256,128]{1,0:T(8,128)(2,1)S(1)} %copy-done.1, bf16[2,256,128]{2,1,0:T(8,128)(2,1)S(1)} %yz_mlp.1.refs_0_), custom_call_target="tpu_custom_call" | custom-call | flops 402653184 | bytes 1048576 | tf_op jit(solution)/shard_map/voxels/pallas_call | solution.py:400
  30.5 0.0 collective-permute-done.7.refs_0_
  30.6 1.1 %voxels.7 = (bf16[6,256,16,128]{3,2,1,0:T(8,128)(2,1)}, bf16[2,6,16,16,128]{4,3,2,1,0:T(8,128)(2,1)S(1)}) custom-call(s32[1]{0:T(128)} %bitcast.me_ref, f32[16,6,256,256]{3,2,1,0:T(8,128)S(1)} %first_layer.1.first_ref, bf16[128,256]{1,0:T(8,128)(2,1)S(1)} %copy-done, bf16[256,128]{1,0:T(8,128)(2,1)S(1)} %copy-done.1, ...), custom_call_target="tpu_custom_call", output_to_operand_aliasing={{0}: (6, {})} | custom-call | flops 402653184 | bytes 1048576 | tf_op jit(solution)/shard_map/voxels/pallas_call | solution.py:400
  31.6 1.1 %collective-permute-done.6.refs_0_ = bf16[2,256,128]{2,1,0:T(8,128)(2,1)S(1)} collective-permute-done((bf16[2,256,128]{2,1,0:T(8,128)(2,1)S(1)}, bf16[2,256,128]{2,1,0:T(8,128)(2,1)S(1)}, u32[]{:S(2)}, u32[]{:S(2)}) %collective-permute-start.6) | collective-permute-done | bytes 131104 | tf_op jit(solution)/shard_map/ppermute | solution.py:420
  32.7 0.7 %collective-permute-start.8 = (bf16[2,256,128]{2,1,0:T(8,128)(2,1)S(1)}, bf16[2,256,128]{2,1,0:T(8,128)(2,1)S(1)}, u32[]{:S(2)}, u32[]{:S(2)}) collective-permute-start(bf16[2,256,128]{2,1,0:T(8,128)(2,1)S(1)} %collective-permute-done.6.refs_0_), channel_id=1, source_target_pairs={{0,1},{1,0},{2,3},{3,2},{4,5},{5,4},{6,7},{7,6},{8,9},{9,8},{10,11... | collective-permute-start | bytes 393224 | tf_op jit(solution)/shard_map/ppermute | solution.py:420
  33.4 1.3 %collective-permute-start.5 = (bf16[2,256,128]{2,1,0:T(8,128)(2,1)S(1)}, bf16[2,256,128]{2,1,0:T(8,128)(2,1)S(1)}, u32[]{:S(2)}, u32[]{:S(2)}) collective-permute-start(bf16[2,256,128]{2,1,0:T(8,128)(2,1)S(1)} %yz_mlp.1.refs_0_), channel_id=1, source_target_pairs={{0,7},{1,6},{2,5},{3,4},{4,3},{5,2},{6,1},{7,0},{8,15},{9,14},{10,... | collective-permute-start | bytes 393224 | tf_op jit(solution)/shard_map/ppermute | solution.py:420
  34.7 1.1 %voxels.8 = (bf16[6,256,16,128]{3,2,1,0:T(8,128)(2,1)}, bf16[2,6,16,16,128]{4,3,2,1,0:T(8,128)(2,1)S(1)}) custom-call(s32[1]{0:T(128)} %bitcast.me_ref, f32[16,6,256,256]{3,2,1,0:T(8,128)S(1)} %first_layer.1.first_ref, bf16[128,256]{1,0:T(8,128)(2,1)S(1)} %copy-done, bf16[256,128]{1,0:T(8,128)(2,1)S(1)} %copy-done.1, ...), custom_call_target="tpu_custom_call", output_to_operand_aliasing={{0}: (6, {})} | custom-call | flops 402653184 | bytes 1048576 | tf_op jit(solution)/shard_map/voxels/pallas_call | solution.py:400
  35.8 0.0 collective-permute-done.9.refs_1_
  35.8 0.6 %collective-permute-start.11 = (bf16[2,256,128]{2,1,0:T(8,128)(2,1)S(1)}, bf16[2,256,128]{2,1,0:T(8,128)(2,1)S(1)}, u32[]{:S(2)}, u32[]{:S(2)}) collective-permute-start(bf16[2,256,128]{2,1,0:T(8,128)(2,1)S(1)} %collective-permute-done.9.refs_1_), channel_id=1, source_target_pairs={{0,1},{1,0},{2,3},{3,2},{4,5},{5,4},{6,7},{7,6},{8,9},{9,8},{10,11... | collective-permute-start | bytes 393224 | tf_op jit(solution)/shard_map/ppermute | solution.py:420
  36.4 0.0 collective-permute-done.8.refs_0_
  36.4 2.0 %voxels.9 = (bf16[6,256,16,128]{3,2,1,0:T(8,128)(2,1)}, bf16[4,6,16,16,128]{4,3,2,1,0:T(8,128)(2,1)S(1)}) custom-call(s32[1]{0:T(128)} %bitcast.me_ref, f32[16,6,256,256]{3,2,1,0:T(8,128)S(1)} %first_layer.1.first_ref, bf16[128,256]{1,0:T(8,128)(2,1)S(1)} %copy-done, bf16[256,128]{1,0:T(8,128)(2,1)S(1)} %copy-done.1, ...), custom_call_target="tpu_custom_call", output_to_operand_aliasing={{0}: (7, {})} | custom-call | flops 805306368 | bytes 1048576 | tf_op jit(solution)/shard_map/voxels/pallas_call | solution.py:400
  38.4 1.6 %collective-permute-done.5.refs_1_ = bf16[2,256,128]{2,1,0:T(8,128)(2,1)S(1)} collective-permute-done((bf16[2,256,128]{2,1,0:T(8,128)(2,1)S(1)}, bf16[2,256,128]{2,1,0:T(8,128)(2,1)S(1)}, u32[]{:S(2)}, u32[]{:S(2)}) %collective-permute-start.5) | collective-permute-done | bytes 131104 | tf_op jit(solution)/shard_map/ppermute | solution.py:420
  40.0 0.1 collective-permute-start.10
  40.1 0.0 collective-permute-done.11.refs_0_
  40.1 2.0 %voxels.10 = (bf16[6,256,16,128]{3,2,1,0:T(8,128)(2,1)}, bf16[4,6,16,16,128]{4,3,2,1,0:T(8,128)(2,1)S(1)}) custom-call(s32[1]{0:T(128)} %bitcast.me_ref, f32[16,6,256,256]{3,2,1,0:T(8,128)S(1)} %first_layer.1.first_ref, bf16[128,256]{1,0:T(8,128)(2,1)S(1)} %copy-done, bf16[256,128]{1,0:T(8,128)(2,1)S(1)} %copy-done.1, ...), custom_call_target="tpu_custom_call", output_to_operand_aliasing={{0}: (7, {})} | custom-call | flops 805306368 | bytes 1048576 | tf_op jit(solution)/shard_map/voxels/pallas_call | solution.py:400
  42.1 0.0 collective-permute-done.10.refs_0_
  42.1 1.8 %voxels.11 = bf16[6,256,16,128]{3,2,1,0:T(8,128)(2,1)} custom-call(s32[1]{0:T(128)} %bitcast.me_ref, f32[16,6,256,256]{3,2,1,0:T(8,128)S(1)} %first_layer.1.first_ref, bf16[128,256]{1,0:T(8,128)(2,1)S(1)} %copy-done, bf16[256,128]{1,0:T(8,128)(2,1)S(1)} %copy-done.1, ...), custom_call_target="tpu_custom_call", output_to_operand_aliasing={{}: (6, {})} | custom-call | flops 402653184 | bytes 1048576 | tf_op jit(solution)/shard_map/voxels/pallas_call | solution.py:400
  (7 shorter events, 0.0 us)
Async XLA Ops:
  3.6 2.3 %collective-permute-start = (bf16[8,272,128]{2,1,0:T(8,128)(2,1)S(1)}, bf16[8,272,128]{2,1,0:T(8,128)(2,1)S(1)}, u32[]{:S(2)}, u32[]{:S(2)}) collective-permute-start(bf16[8,272,128]{2,1,0:T(8,128)(2,1)S(1)} %get-tuple-element.47), channel_id=1, source_target_pairs={{0,1},{1,0},{2,3},{3,2},{4,5},{5,4},{6,7},{7,6},{8,9},{9,8},{10,11... | collective-permute-start | bytes 1671176 | tf_op jit(solution)/shard_map/ppermute | solution.py:420
  5.9 7.9 %copy-start.4 = (bf16[128,512]{1,0:T(8,128)(2,1)S(1)}, bf16[128,512]{1,0:T(8,128)(2,1)}, u32[]{:S(2)}) copy-start(bf16[128,512]{1,0:T(8,128)(2,1)} %xy_in.1) | copy-start | bytes 393220
  5.9 7.9 %copy-start.5 = (bf16[512,128]{1,0:T(8,128)(2,1)S(1)}, bf16[512,128]{1,0:T(8,128)(2,1)}, u32[]{:S(2)}) copy-start(bf16[512,128]{1,0:T(8,128)(2,1)} %xy_out.1) | copy-start | bytes 393220
  5.9 7.9 %copy-start.6 = (bf16[128,512]{1,0:T(8,128)(2,1)S(1)}, bf16[128,512]{1,0:T(8,128)(2,1)}, u32[]{:S(2)}) copy-start(bf16[128,512]{1,0:T(8,128)(2,1)} %xz_in.1) | copy-start | bytes 393220
  5.9 7.9 %copy-start.7 = (bf16[512,128]{1,0:T(8,128)(2,1)S(1)}, bf16[512,128]{1,0:T(8,128)(2,1)}, u32[]{:S(2)}) copy-start(bf16[512,128]{1,0:T(8,128)(2,1)} %xz_out.1) | copy-start | bytes 393220
  5.9 14.0 %copy-start = (bf16[128,256]{1,0:T(8,128)(2,1)S(1)}, bf16[128,256]{1,0:T(8,128)(2,1)}, u32[]{:S(2)}) copy-start(bf16[128,256]{1,0:T(8,128)(2,1)} %w_in.13) | copy-start | bytes 196612
  6.2 9.4 %collective-permute-start.3 = (bf16[2,272,128]{2,1,0:T(8,128)(2,1)S(1)}, bf16[2,272,128]{2,1,0:T(8,128)(2,1)S(1)}, u32[]{:S(2)}, u32[]{:S(2)}) collective-permute-start(bf16[2,272,128]{2,1,0:T(8,128)(2,1)S(1)} %get-tuple-element.83), channel_id=1, source_target_pairs={{0,7},{1,6},{2,5},{3,4},{4,3},{5,2},{6,1},{7,0},{8,15},{9,14},{10,... | collective-permute-start | bytes 417800 | tf_op jit(solution)/shard_map/ppermute | solution.py:420
  9.9 6.9 %collective-permute-start.2 = (bf16[2,272,128]{2,1,0:T(8,128)(2,1)S(1)}, bf16[2,272,128]{2,1,0:T(8,128)(2,1)S(1)}, u32[]{:S(2)}, u32[]{:S(2)}) collective-permute-start(bf16[2,272,128]{2,1,0:T(8,128)(2,1)S(1)} %get-tuple-element.84), channel_id=1, source_target_pairs={{0,5},{1,4},{2,7},{3,6},{4,1},{5,0},{6,3},{7,2},{8,13},{9,12},{10,... | collective-permute-start | bytes 417800 | tf_op jit(solution)/shard_map/ppermute | solution.py:420
  10.1 7.0 %collective-permute-start.1 = (bf16[2,272,128]{2,1,0:T(8,128)(2,1)S(1)}, bf16[2,272,128]{2,1,0:T(8,128)(2,1)S(1)}, u32[]{:S(2)}, u32[]{:S(2)}) collective-permute-start(bf16[2,272,128]{2,1,0:T(8,128)(2,1)S(1)} %get-tuple-element.85), channel_id=1, source_target_pairs={{0,3},{1,2},{2,1},{3,0},{4,7},{5,6},{6,5},{7,4},{8,11},{9,10},{10,... | collective-permute-start | bytes 417800 | tf_op jit(solution)/shard_map/ppermute | solution.py:420
  17.1 9.8 %collective-permute-start.4 = (bf16[2,272,128]{2,1,0:T(8,128)(2,1)S(1)}, bf16[2,272,128]{2,1,0:T(8,128)(2,1)S(1)}, u32[]{:S(2)}, u32[]{:S(2)}) collective-permute-start(bf16[2,272,128]{2,1,0:T(8,128)(2,1)S(1)} %add_convert_fusion.1.refs_0_), channel_id=1, source_target_pairs={{0,8},{1,9},{2,10},{3,11},{4,12},{5,13},{6,14},{7,15},{8,0},{9,1},... | collective-permute-start | bytes 417800 | tf_op jit(solution)/shard_map/ppermute | solution.py:420
  19.9 6.9 %copy-start.2 = (bf16[128,512]{1,0:T(8,128)(2,1)S(1)}, bf16[128,512]{1,0:T(8,128)(2,1)}, u32[]{:S(2)}) copy-start(bf16[128,512]{1,0:T(8,128)(2,1)} %refs_2_.1) | copy-start | bytes 393220
  19.9 6.9 %copy-start.3 = (bf16[512,128]{1,0:T(8,128)(2,1)S(1)}, bf16[512,128]{1,0:T(8,128)(2,1)}, u32[]{:S(2)}) copy-start(bf16[512,128]{1,0:T(8,128)(2,1)} %refs_3_.1) | copy-start | bytes 393220
  19.9 9.5 %copy-start.1 = (bf16[256,128]{1,0:T(8,128)(2,1)S(1)}, bf16[256,128]{1,0:T(8,128)(2,1)}, u32[]{:S(2)}) copy-start(bf16[256,128]{1,0:T(8,128)(2,1)} %w_out.11) | copy-start | bytes 196612
  27.4 3.2 %collective-permute-start.7 = (bf16[2,256,128]{2,1,0:T(8,128)(2,1)S(1)}, bf16[2,256,128]{2,1,0:T(8,128)(2,1)S(1)}, u32[]{:S(2)}, u32[]{:S(2)}) collective-permute-start(bf16[2,256,128]{2,1,0:T(8,128)(2,1)S(1)} %yz_mlp.1.refs_0_), channel_id=1, source_target_pairs={{0,1},{1,0},{2,3},{3,2},{4,5},{5,4},{6,7},{7,6},{8,9},{9,8},{10,11... | collective-permute-start | bytes 393224 | tf_op jit(solution)/shard_map/ppermute | solution.py:420
  27.5 5.2 %collective-permute-start.6 = (bf16[2,256,128]{2,1,0:T(8,128)(2,1)S(1)}, bf16[2,256,128]{2,1,0:T(8,128)(2,1)S(1)}, u32[]{:S(2)}, u32[]{:S(2)}) collective-permute-start(bf16[2,256,128]{2,1,0:T(8,128)(2,1)S(1)} %yz_mlp.1.refs_0_), channel_id=1, source_target_pairs={{0,3},{1,2},{2,1},{3,0},{4,7},{5,6},{6,5},{7,4},{8,11},{9,10},{10,... | collective-permute-start | bytes 393224 | tf_op jit(solution)/shard_map/ppermute | solution.py:420
  29.1 6.6 %collective-permute-start.9 = (bf16[2,256,128]{2,1,0:T(8,128)(2,1)S(1)}, bf16[2,256,128]{2,1,0:T(8,128)(2,1)S(1)}, u32[]{:S(2)}, u32[]{:S(2)}) collective-permute-start(bf16[2,256,128]{2,1,0:T(8,128)(2,1)S(1)} %yz_mlp.1.refs_0_), channel_id=1, source_target_pairs={{0,5},{1,4},{2,7},{3,6},{4,1},{5,0},{6,3},{7,2},{8,13},{9,12},{10,... | collective-permute-start | bytes 393224 | tf_op jit(solution)/shard_map/ppermute | solution.py:420
  32.7 3.7 %collective-permute-start.8 = (bf16[2,256,128]{2,1,0:T(8,128)(2,1)S(1)}, bf16[2,256,128]{2,1,0:T(8,128)(2,1)S(1)}, u32[]{:S(2)}, u32[]{:S(2)}) collective-permute-start(bf16[2,256,128]{2,1,0:T(8,128)(2,1)S(1)} %collective-permute-done.6.refs_0_), channel_id=1, source_target_pairs={{0,1},{1,0},{2,3},{3,2},{4,5},{5,4},{6,7},{7,6},{8,9},{9,8},{10,11... | collective-permute-start | bytes 393224 | tf_op jit(solution)/shard_map/ppermute | solution.py:420
  33.4 6.5 %collective-permute-start.5 = (bf16[2,256,128]{2,1,0:T(8,128)(2,1)S(1)}, bf16[2,256,128]{2,1,0:T(8,128)(2,1)S(1)}, u32[]{:S(2)}, u32[]{:S(2)}) collective-permute-start(bf16[2,256,128]{2,1,0:T(8,128)(2,1)S(1)} %yz_mlp.1.refs_0_), channel_id=1, source_target_pairs={{0,7},{1,6},{2,5},{3,4},{4,3},{5,2},{6,1},{7,0},{8,15},{9,14},{10,... | collective-permute-start | bytes 393224 | tf_op jit(solution)/shard_map/ppermute | solution.py:420
  35.8 4.3 %collective-permute-start.11 = (bf16[2,256,128]{2,1,0:T(8,128)(2,1)S(1)}, bf16[2,256,128]{2,1,0:T(8,128)(2,1)S(1)}, u32[]{:S(2)}, u32[]{:S(2)}) collective-permute-start(bf16[2,256,128]{2,1,0:T(8,128)(2,1)S(1)} %collective-permute-done.9.refs_1_), channel_id=1, source_target_pairs={{0,1},{1,0},{2,3},{3,2},{4,5},{5,4},{6,7},{7,6},{8,9},{9,8},{10,11... | collective-permute-start | bytes 393224 | tf_op jit(solution)/shard_map/ppermute | solution.py:420
  40.0 2.1 %collective-permute-start.10 = (bf16[2,256,128]{2,1,0:T(8,128)(2,1)S(1)}, bf16[2,256,128]{2,1,0:T(8,128)(2,1)S(1)}, u32[]{:S(2)}, u32[]{:S(2)}) collective-permute-start(bf16[2,256,128]{2,1,0:T(8,128)(2,1)S(1)} %collective-permute-done.5.refs_1_), channel_id=1, source_target_pairs={{0,1},{1,0},{2,3},{3,2},{4,5},{5,4},{6,7},{7,6},{8,9},{9,8},{10,11... | collective-permute-start | bytes 393224 | tf_op jit(solution)/shard_map/ppermute | solution.py:420
